TPU v7x, 32 devices: a whole 2x2x4 slice. The times are simulated.
32 devices in a mesh: grp: 1, dev: 32 (over z, y, x, core).
Axes of the slice: x: 2, y: 2, z: 4, core: 2. Of those that a mesh axis runs over, the one named last changes fastest.
Arguments:
- hidden_in: bfloat16 [640, 32, 768], P(('grp', 'dev')), may hold values from -6 to 6
- grad_out: bfloat16 [640, 32, 768], P(('grp', 'dev')), may hold values from -6 to 6
- norm_gain: float32 [768], replicated, may hold values from 0.25 to 1.75
- w_qkv: bfloat16 [768, 2304], replicated, may hold values from -0.21875 to 0.21875
- w_out: bfloat16 [768, 768], replicated, may hold values from -0.21875 to 0.21875
- sharpness: float32 [12], replicated, may hold values from 4 to 20
- cohort_ids: int32 [640], P('grp'), may hold values from 0 to 3
- observed: int32 [640, 32], P('grp', 'dev'), may hold values 0 or 1
Outputs:
- grad_in: bfloat16 [640, 32, 768], P(('grp', 'dev'))
- grad_qkv: float32 [768, 2304], P(('grp', 'dev'))
- grad_wout: float32 [768, 768], P(('grp', 'dev'))
All inputs are finite; a program needn't handle non-finite values. No bound on the sum of `observed` on one device may be relied on, other than what follows from the above.
Results may differ from a plain program's by a relative error of at most 0.015.
Values may be sent and summed in bfloat16 or wider, within the bound.
A program may use at most 128 MiB of HBM per device.

v0:
```python
import jax
import jax.numpy as jnp
from jax import lax
from jax.sharding import PartitionSpec as P

epsilon = 1e-06


def row_sum(left, right):
    return lax.dot_general(
        left, right, (((0,), (0,)), ((), ())), preferred_element_type=jnp.float32
    )


def forward_part(rows_in, norm_gain, w_qkv, heads):
    campaigns, patches, width = rows_in.shape
    head_size = width // heads
    values = rows_in.astype(jnp.float32)
    inv_rms = lax.rsqrt(jnp.mean(values * values, axis=-1, keepdims=True) + epsilon)
    unit_rows = values * inv_rms
    normed = (unit_rows * norm_gain).astype(jnp.bfloat16).reshape(-1, width)
    projected = jnp.dot(normed, w_qkv, preferred_element_type=jnp.float32)
    shape4 = (campaigns, patches, heads, head_size)
    query_raw = projected[:, :width].reshape(shape4)
    key_raw = projected[:, width : 2 * width].reshape(shape4)
    value_half = projected[:, 2 * width :].reshape(shape4).astype(jnp.bfloat16)
    query_inv = lax.rsqrt(jnp.mean(query_raw * query_raw, axis=-1, keepdims=True) + epsilon)
    key_inv = lax.rsqrt(jnp.mean(key_raw * key_raw, axis=-1, keepdims=True) + epsilon)
    query_unit = query_raw * query_inv
    key_unit = key_raw * key_inv
    return (
        inv_rms,
        unit_rows,
        normed,
        query_unit,
        query_inv,
        key_unit,
        key_inv,
        query_unit.astype(jnp.bfloat16),
        key_unit.astype(jnp.bfloat16),
        value_half,
    )


def body(hidden_in, grad_out, norm_gain, w_qkv, w_out, sharpness, cohort_ids, observed):
    heads = sharpness.shape[0]
    rows_in, grad_rows = (
        lax.all_to_all(hidden_in, "dev", split_axis=1, concat_axis=0, tiled=True),
        lax.all_to_all(grad_out, "dev", split_axis=1, concat_axis=0, tiled=True),
    )
    forward = forward_part(rows_in, norm_gain, w_qkv, heads)
    (
        inv_rms,
        unit_rows,
        normed,
        query_unit,
        query_inv,
        key_unit,
        key_inv,
        query_half,
        key_half,
        value_half,
    ) = forward
    campaigns, patches, width = rows_in.shape
    head_size = width // heads
    shape4 = (campaigns, patches, heads, head_size)
    dy_rows = grad_rows.reshape(-1, width)
    grad_attn = lax.dot_general(
        dy_rows, w_out, (((1,), (1,)), ((), ())), preferred_element_type=jnp.float32
    )
    grad_attn = grad_attn.astype(jnp.bfloat16).reshape(shape4)
    same = cohort_ids[:, None] == cohort_ids[None, :]
    diagonal = jnp.eye(campaigns, dtype=bool)
    keys_seen = (observed.T == 1)[:, None, :]
    allowed = jnp.where(same[None] & (keys_seen | diagonal[None]), 1.0, 0.0).astype(jnp.float32)

    def head_step(index, carry):
        attended, grad_qunit, grad_kunit, grad_value = carry
        query_head = lax.dynamic_index_in_dim(query_half, index, 2, keepdims=False)
        key_head = lax.dynamic_index_in_dim(key_half, index, 2, keepdims=False)
        value_head = lax.dynamic_index_in_dim(value_half, index, 2, keepdims=False)
        grad_head = lax.dynamic_index_in_dim(grad_attn, index, 2, keepdims=False)
        scale = lax.dynamic_index_in_dim(sharpness, index, 0, keepdims=False) / head_size
        scores = (
            jnp.einsum("ipe,jpe->pij", query_head, key_head, preferred_element_type=jnp.float32)
            * scale
        )
        raw_weights = jnp.exp(scores) * allowed
        probs = raw_weights / jnp.sum(raw_weights, axis=-1, keepdims=True)
        probs_half = probs.astype(jnp.bfloat16)
        out_head = jnp.einsum(
            "pij,jpe->ipe", probs_half, value_head, preferred_element_type=jnp.float32
        )
        grad_probs = jnp.einsum(
            "ipe,jpe->pij", grad_head, value_head, preferred_element_type=jnp.float32
        )
        value_grad = jnp.einsum(
            "pij,ipe->jpe", probs_half, grad_head, preferred_element_type=jnp.float32
        )
        row_dot = jnp.sum(grad_probs * probs, axis=-1, keepdims=True)
        grad_scores = (probs * (grad_probs - row_dot) * scale).astype(jnp.bfloat16)
        qunit_head = jnp.einsum(
            "pij,jpe->ipe", grad_scores, key_head, preferred_element_type=jnp.float32
        )
        kunit_head = jnp.einsum(
            "pij,ipe->jpe", grad_scores, query_head, preferred_element_type=jnp.float32
        )
        return (
            lax.dynamic_update_index_in_dim(attended, out_head, index, 2),
            lax.dynamic_update_index_in_dim(grad_qunit, qunit_head, index, 2),
            lax.dynamic_update_index_in_dim(grad_kunit, kunit_head, index, 2),
            lax.dynamic_update_index_in_dim(grad_value, value_grad, index, 2),
        )

    empty = jnp.zeros(shape4, jnp.float32)
    attended, grad_qunit, grad_kunit, grad_value = lax.fori_loop(
        0, heads, head_step, (empty, empty, empty, empty)
    )
    grad_query = query_inv * (
        grad_qunit - query_unit * jnp.mean(grad_qunit * query_unit, axis=-1, keepdims=True)
    )
    grad_key = key_inv * (
        grad_kunit - key_unit * jnp.mean(grad_kunit * key_unit, axis=-1, keepdims=True)
    )
    grad_proj = jnp.concatenate(
        [grad_query.reshape(-1, width), grad_key.reshape(-1, width), grad_value.reshape(-1, width)],
        axis=1,
    ).astype(jnp.bfloat16)
    attended_half = attended.astype(jnp.bfloat16).reshape(-1, width)
    out_term = row_sum(attended_half, dy_rows)
    grad_wout = lax.psum_scatter(
        out_term.astype(jnp.bfloat16), "dev", scatter_dimension=0, tiled=True
    ).astype(jnp.float32)
    grad_normed = lax.dot_general(
        grad_proj, w_qkv, (((1,), (1,)), ((), ())), preferred_element_type=jnp.float32
    )
    shaped = grad_normed.reshape(campaigns, patches, width) * norm_gain
    result = grad_rows.astype(jnp.float32) + inv_rms * (
        shaped - unit_rows * jnp.mean(shaped * unit_rows, axis=-1, keepdims=True)
    )
    grad_in = lax.all_to_all(
        result.astype(jnp.bfloat16), "dev", split_axis=0, concat_axis=1, tiled=True
    )
    grad_qkv = lax.psum_scatter(
        row_sum(normed, grad_proj).astype(jnp.bfloat16), "dev", scatter_dimension=0, tiled=True
    ).astype(jnp.float32)
    return (grad_in, grad_qkv, grad_wout)


def solution(mesh):
    in_specs = (
        P(("grp", "dev"), None, None),
        P(("grp", "dev"), None, None),
        P(),
        P(),
        P(),
        P(),
        P("grp"),
        P("grp", "dev"),
    )
    out_specs = (P(("grp", "dev"), None, None), P(("grp", "dev"), None), P(("grp", "dev"), None))
    return jax.shard_map(body, mesh=mesh, in_specs=in_specs, out_specs=out_specs, check_vma=False)
```

profile of v0, /device:TPU:0, one launch (start us, length us, event | category | flops | bytes accessed | tf_op | source)
XLA Modules:
  0.0 459.8 jit_solution(5012240428037647978)
XLA Ops:
  7.2 2.9 copy.28
  10.1 7.4 %all-to-all-start.1 = ((bf16[20,32,768]{2,0,1:T(8,128)(2,1)}), bf16[20,32,768]{2,0,1:T(8,128)(2,1)}, u32[]{:S(2)}, u32[]{:S(2)}) async-start(bf16[20,32,768]{2,0,1:T(8,128)(2,1)} %copy.28), calls=%async_computation.1 | async-start | bytes 2359296 | tf_op jit(solution)/shard_map/all_to_all | solution.py:48
  17.6 2.8 copy.27
  21.0 25.6 %all-to-all-done.1 = bf16[20,32,768]{2,0,1:T(8,128)(2,1)} async-done(((bf16[20,32,768]{2,0,1:T(8,128)(2,1)}), bf16[20,32,768]{2,0,1:T(8,128)(2,1)}, u32[]{:S(2)}, u32[]{:S(2)}) %all-to-all-start.1) | async-done | bytes 983072 | tf_op jit(solution)/shard_map/all_to_all | solution.py:48
  46.5 3.7 all-to-all-start
  52.6 2.9 convert_bitcast_fusion
  56.1 2.7 reshape.437
  60.3 4.1 fusion.38
  65.4 2.3 fusion.40
  67.7 2.9 copy.33
  70.5 2.9 copy.31
  73.4 2.2 copy.32
  79.3 2.1 all_to_all.36
  81.4 3.5 convolution_convert_fusion.2
  85.0 2.2 copy.34
  87.2 3.9 multiply_convert_fusion.4
  91.1 145.6 %while.20 = (s32[]{:T(128)}, bf16[640,1,12,64]{0,3,2,1:T(8,128)(2,1)}, f32[640,1,12,64]{0,3,2,1:T(8,128)}, f32[640,1,12,64]{0,3,2,1:T(8,128)}, bf16[640,1,12,64]...) while((s32[]{:T(128)}, ...), condition=%wide.region_6.7_spmd.clone, body=%wide.region_3.6_spmd.clone.sunk | while | flops 322763520 | bytes 15271073 | solution.py:116
  180.7 2.0 fusion.73
  236.8 3.2 multiply_reduce_fusion.3
  241.3 3.3 convolution_convert_fusion.1
  246.4 2.7 multiply_convert_fusion.2
  252.0 6.2 %convolution_convert_fusion = bf16[768,2304]{1,0:T(8,128)(2,1)} fusion(bf16[640,768]{0,1:T(8,128)(2,1)} %bitcast.11, bf16[640,768]{0,1:T(8,128)(2,1)S(1)} %bitcast.138, bf16[640,768]{0,1:T(8,128)(2,1)S(1)} %bitcast.136, f32[640,768]{1,0:T(8,128)S(1)} %copy-done.4, f32[768]{0:T(1024)S(1)} %copy-done.16, f32[640]{0:T(1024)S(1)} %copy-done.15), kind=kOutput, calls=%fused_computation.41 | convolution fusion | flops 2277015552 | bytes 8459776 | tf_op jit(solution)/shard_map/dot_general | solution.py:10
  258.3 5.5 %multiply_reduce_fusion.1 = (f32[640]{0:T(1024)S(1)}, f32[640,768]{1,0:T(8,128)S(1)}) fusion(f32[640,768]{1,0:T(8,128)} %reshape.437, f32[768]{0:T(1024)S(1)} %copy-done.16, f32[640]{0:T(1024)S(1)} %copy-done.15, bf16[768,2304]{1,0:T(8,128)(2,1)S(1)} %copy-done, bf16[640,768]{0,1:T(8,128)(2,1)} %bitcast.11, bf16[640,768]{0,1:T(8,128)(2,1)} %bitcast.139, ...), kind=kOutput, calls=%fused_computation.48 | convolution fusion | flops 2275737088 | bytes 10428416 | tf_op jit(solution)/shard_map/dot_general | solution.py:134
  265.8 3.3 reduce.21
  269.0 3.3 reshape.446
  272.3 6.0 %all-to-all-start.2 = ((bf16[32,2,7680]{2,1,0:T(2,128)(2,1)}), bf16[32,2,7680]{2,1,0:T(2,128)(2,1)}, u32[]{:S(2)}, u32[]{:S(2)}) async-start(bf16[32,2,7680]{2,1,0:T(2,128)(2,1)} %reshape.446), calls=%async_computation.2 | async-start | bytes 1966080 | tf_op jit(solution)/shard_map/all_to_all | solution.py:141
  278.3 65.1 %reduce-scatter.5.cloned.1.call-done = bf16[24,768]{1,0:T(8,128)(2,1)} async-done(((bf16[768,768]{1,0:T(8,128)(2,1)}), bf16[24,768]{1,0:T(8,128)(2,1)}) %reduce-scatter.5.cloned.1.call-update) | async-done | bytes 36880 | tf_op jit(solution)/shard_map/reduce_scatter | solution.py:131
  344.8 5.6 %reshape.447 = bf16[640,1,768]{2,1,0:T(2,128)(2,1)} reshape(bf16[32,2,7680]{2,1,0:T(2,128)(2,1)} %all-to-all-done.2) | data formatting | bytes 1966080
  350.5 7.9 %reduce.19 = bf16[640,768]{1,0:T(8,128)(2,1)} reduce(bf16[640,1,768]{2,1,0:T(2,128)(2,1)} %reshape.447, bf16[]{:T(256)} %constant.84), dimensions={1}, to_apply=%all_to_all.38.reduce_sub_computation | reduce | bytes 1966082 | tf_op jit(solution)/shard_map/all_to_all | solution.py:141
  358.4 2.2 all_to_all.39
  360.6 2.4 copy.36
  363.0 88.4 %reduce-scatter.3.cloned.1.call-done = bf16[24,2304]{1,0:T(8,128)(2,1)} async-done(((bf16[768,2304]{1,0:T(8,128)(2,1)}), bf16[24,2304]{1,0:T(8,128)(2,1)}) %reduce-scatter.3.cloned.1.call-update) | async-done | bytes 110608 | tf_op jit(solution)/shard_map/reduce_scatter | solution.py:144
  (167 shorter events, 156.6 us)
Async XLA Ops:
  7.2 53.1 %copy-start = (bf16[768,2304]{1,0:T(8,128)(2,1)S(1)}, bf16[768,2304]{1,0:T(8,128)(2,1)}, u32[]{:S(2)}) copy-start(bf16[768,2304]{1,0:T(8,128)(2,1)} %param.13) | copy-start | bytes 10616836
  10.1 10.3 %copy-start.17 = (s32[640,1]{0,1:T(1,128)S(1)}, s32[640,1]{0,1:T(1,128)}, u32[]{:S(2)}) copy-start(s32[640,1]{0,1:T(1,128)} %param.17) | copy-start | bytes 7684
  10.1 36.5 %all-to-all-start.1 = ((bf16[20,32,768]{2,0,1:T(8,128)(2,1)}), bf16[20,32,768]{2,0,1:T(8,128)(2,1)}, u32[]{:S(2)}, u32[]{:S(2)}) async-start(bf16[20,32,768]{2,0,1:T(8,128)(2,1)} %copy.28), calls=%async_computation.1 | async-start | bytes 2359296 | tf_op jit(solution)/shard_map/all_to_all | solution.py:48
  46.5 32.7 %all-to-all-start = ((bf16[20,32,768]{2,0,1:T(8,128)(2,1)}), bf16[20,32,768]{2,0,1:T(8,128)(2,1)}, u32[]{:S(2)}, u32[]{:S(2)}) async-start(bf16[20,32,768]{2,0,1:T(8,128)(2,1)} %copy.27), calls=%async_computation | async-start | bytes 2359296 | tf_op jit(solution)/shard_map/all_to_all | solution.py:49
  50.3 293.1 %reduce-scatter.5.cloned.1.call-start = ((), (), s32[]{:S(2)}) async-start(), calls=%async_computation.6 | async-start | bytes 1216512 | tf_op jit(solution)/shard_map/reduce_scatter | solution.py:131
  52.6 2.9 copy-start.14
  75.6 2.1 copy-start.3
  87.2 3.9 copy-start.18
  87.2 3.9 copy-start.19
  87.2 3.9 copy-start.20
  236.7 3.2 copy-start.1
  236.8 3.3 copy-start.6
  236.8 3.3 copy-start.12
  240.1 1.2 copy-start.8
  244.6 206.7 %reduce-scatter.3.cloned.1.call-start = ((), (), s32[]{:S(2)}) async-start(), calls=%async_computation.5 | async-start | bytes 3649536 | tf_op jit(solution)/shard_map/reduce_scatter | solution.py:144
  246.4 2.7 copy-start.2
  246.4 3.3 copy-start.7
  246.4 3.3 copy-start.13
  249.8 1.0 copy-start.10
  249.8 2.3 copy-start.4
  249.8 2.3 copy-start.15
  249.8 2.3 copy-start.16
  250.2 0.9 copy-start.11
  258.2 5.5 %copy-start.5 = (f32[640,768]{1,0:T(8,128)S(1)}, f32[640,768]{1,0:T(8,128)}, u32[]{:S(2)}) copy-start(f32[640,768]{1,0:T(8,128)} %reshape.437) | copy-start | bytes 5898244
  258.2 5.5 %copy-start.9 = (bf16[640,768]{1,0:T(8,128)(2,1)S(1)}, bf16[640,768]{1,0:T(8,128)(2,1)}, u32[]{:S(2)}) copy-start(bf16[640,768]{1,0:T(8,128)(2,1)} %all_to_all.36) | copy-start | bytes 2949124
  272.3 72.6 %all-to-all-start.2 = ((bf16[32,2,7680]{2,1,0:T(2,128)(2,1)}), bf16[32,2,7680]{2,1,0:T(2,128)(2,1)}, u32[]{:S(2)}, u32[]{:S(2)}) async-start(bf16[32,2,7680]{2,1,0:T(2,128)(2,1)} %reshape.446), calls=%async_computation.2 | async-start | bytes 1966080 | tf_op jit(solution)/shard_map/all_to_all | solution.py:141
Sparse Core Ops, SparseCore 0:
  244.8 98.6 reduce-scatter.4
  348.8 102.4 reduce-scatter.2
where the time goes:
time: 464 us; the launch traced here: 460 us
  waiting for transfers between devices  179 us (39%)
  matrix products  149 us (32%)
  local copies, waits for them, and re-layouts  50.9 us (11%)
  other arithmetic  41.2 us (9%)
  starting transfers between devices  17.5 us (4%)
  between operations  14.2 us (3%)
  loops' own time  7.86 us (2%)
    reduce_scatter x1, waiting for transfers between devices, body(): lax.psum_scatter(row_sum(normed, grad_proj).astype(jnp.bfloat16), 'dev',...  88.4 us
    reduce_scatter x1, waiting for transfers between devices, body(): lax.psum_scatter(out_term.astype(jnp.bfloat16), 'dev', scatter_dimension=...  65.1 us
    all_to_all x1, waiting for transfers between devices, body(): lax.all_to_all(hidden_in, 'dev', split_axis=1, concat_axis=0, tiled=True)  25.6 us
    dot_general x12, matrix products, head_step(): jnp.einsum('pij,ipe->jpe', grad_scores, query_head, preferred_element_typ...  23.3 us
    dot_general x12, matrix products, head_step(): jnp.einsum('pij,ipe->jpe', probs_half, grad_head, preferred_element_type=...  22.9 us
    dot_general x12, matrix products, head_step(): jnp.einsum('pij,jpe->ipe', grad_scores, key_head, preferred_element_type=...  21.9 us
    dot_general x12, matrix products, head_step(): jnp.einsum('pij,jpe->ipe', probs_half, value_head, preferred_element_type...  21.6 us
    unnamed x48, local copies, waits for them, and re-layouts  20.8 us
  transfers between devices with their start and end apart: 5, of which 4 were waited for; matrix products, arithmetic and copies ran while one was open for 16% of the time, Pallas kernels for 0%

commit v1 on v0

v1 whole, which is shorter than its diff:
```python
import functools
import math

import jax
import jax.numpy as jnp
from jax import lax
from jax.experimental import pallas as pl
from jax.experimental.pallas import tpu as pltpu
from jax.sharding import PartitionSpec as P

epsilon = 1e-06
log2e = math.log2(math.e)


def dot(left, right, dims):
    return lax.dot_general(left, right, ((dims[0], dims[1]), ((), ())), preferred_element_type=jnp.float32)


def compute_kernel(
    head_size,
    group,
    sharp_ref,
    x_ref,
    dy_ref,
    gain_ref,
    wq_ref,
    wk_ref,
    wv_ref,
    wo_ref,
    cohort_col_ref,
    cohort_row_ref,
    seen_ref,
    gin_ref,
    gqkv_ref,
    gwo_ref,
    normed_ref,
    normed_t_ref,
    mask_ref,
    acc_ref,
    dproj_ref,
    att_ref,
):
    step = pl.program_id(0)
    rows, width = x_ref.shape
    gw = group * head_size

    @pl.when(step == 0)
    def _():
        values = x_ref[...].astype(jnp.float32)
        inv = lax.rsqrt(jnp.mean(values * values, axis=-1, keepdims=True) + epsilon)
        normed = values * inv * gain_ref[...]
        normed_ref[...] = normed.astype(jnp.bfloat16)
        normed_t_ref[...] = normed.T.astype(jnp.bfloat16)
        same = cohort_col_ref[...] == cohort_row_ref[...]
        diagonal = lax.broadcasted_iota(jnp.int32, (rows, rows), 0) == lax.broadcasted_iota(
            jnp.int32, (rows, rows), 1
        )
        seen = jnp.broadcast_to(seen_ref[...], (rows, rows)) == 1
        mask_ref[...] = jnp.where(same & (seen | diagonal), 1.0, 0.0)
        acc_ref[...] = jnp.zeros_like(acc_ref)

    normed = normed_ref[...]
    q_raw = dot(normed, wq_ref[...], ((1,), (0,)))
    k_raw = dot(normed, wk_ref[...], ((1,), (0,)))
    v_half = dot(normed, wv_ref[...], ((1,), (0,))).astype(jnp.bfloat16)
    da_half = dot(dy_ref[...], wo_ref[...], ((1,), (1,))).astype(jnp.bfloat16)
    for h in range(group):
        lanes = slice(h * head_size, (h + 1) * head_size)
        q = q_raw[:, lanes]
        k = k_raw[:, lanes]
        v = v_half[:, lanes]
        da = da_half[:, lanes]
        q_inv = lax.rsqrt(jnp.mean(q * q, axis=-1, keepdims=True) + epsilon)
        k_inv = lax.rsqrt(jnp.mean(k * k, axis=-1, keepdims=True) + epsilon)
        q_unit = q * q_inv
        k_unit = k * k_inv
        q_half = q_unit.astype(jnp.bfloat16)
        k_half = k_unit.astype(jnp.bfloat16)
        k_t = k_unit.T.astype(jnp.bfloat16)
        v_t = v.astype(jnp.float32).T.astype(jnp.bfloat16)
        scale = sharp_ref[step * group + h] / head_size
        scores = dot(k_half, q_half, ((1,), (1,)))
        grad_probs = dot(v, da, ((1,), (1,)))
        weights = jnp.exp2(scores * (scale * log2e)) * mask_ref[...]
        probs = weights * (1.0 / jnp.sum(weights, axis=0, keepdims=True))
        probs_half = probs.astype(jnp.bfloat16)
        att_t = dot(v_t, probs_half, ((1,), (0,)))
        grad_v = dot(probs_half, da, ((1,), (0,)))
        row_dot = jnp.sum(grad_probs * probs, axis=0, keepdims=True)
        grad_scores = (probs * (grad_probs - row_dot)).astype(jnp.bfloat16)
        dq = dot(k_t, grad_scores, ((1,), (0,))).T * scale
        dk = dot(grad_scores, q_half, ((1,), (0,))) * scale
        dq = q_inv * (dq - q_unit * jnp.mean(dq * q_unit, axis=-1, keepdims=True))
        dk = k_inv * (dk - k_unit * jnp.mean(dk * k_unit, axis=-1, keepdims=True))
        base = h * head_size
        dproj_ref[:, base : base + head_size] = dq.astype(jnp.bfloat16)
        dproj_ref[:, gw + base : gw + base + head_size] = dk.astype(jnp.bfloat16)
        dproj_ref[:, 2 * gw + base : 2 * gw + base + head_size] = grad_v.astype(jnp.bfloat16)
        att_ref[base : base + head_size, :] = att_t.astype(jnp.bfloat16)
    gwo_ref[...] = dot(att_ref[...], dy_ref[...], ((1,), (0,))).astype(jnp.bfloat16)
    gqkv_ref[0] = dot(normed_t_ref[...], dproj_ref[...], ((1,), (0,))).astype(jnp.bfloat16)
    acc_ref[...] += (
        dot(dproj_ref[:, :gw], wq_ref[...], ((1,), (1,)))
        + dot(dproj_ref[:, gw : 2 * gw], wk_ref[...], ((1,), (1,)))
        + dot(dproj_ref[:, 2 * gw :], wv_ref[...], ((1,), (1,)))
    )

    @pl.when(step == pl.num_programs(0) - 1)
    def _():
        values = x_ref[...].astype(jnp.float32)
        inv = lax.rsqrt(jnp.mean(values * values, axis=-1, keepdims=True) + epsilon)
        unit = values * inv
        shaped = acc_ref[...] * gain_ref[...]
        result = dy_ref[...].astype(jnp.float32) + inv * (
            shaped - unit * jnp.mean(shaped * unit, axis=-1, keepdims=True)
        )
        gin_ref[...] = result.astype(jnp.bfloat16)


def patch_grads(x, dy, norm_gain, w_qkv, w_out, sharpness, cohort_ids, seen):
    rows, width = x.shape
    heads = sharpness.shape[0]
    head_size = width // heads
    group = math.gcd(heads, 2)
    steps = heads // group
    gw = group * head_size
    whole = lambda shape: pl.BlockSpec(shape, lambda g: (0,) * len(shape))
    return pl.pallas_call(
        functools.partial(compute_kernel, head_size, group),
        grid=(steps,),
        in_specs=[
            pl.BlockSpec(memory_space=pltpu.SMEM),
            whole((rows, width)),
            whole((rows, width)),
            whole((1, width)),
            pl.BlockSpec((width, gw), lambda g: (0, g)),
            pl.BlockSpec((width, gw), lambda g: (0, steps + g)),
            pl.BlockSpec((width, gw), lambda g: (0, 2 * steps + g)),
            pl.BlockSpec((gw, width), lambda g: (g, 0)),
            whole((rows, 1)),
            whole((1, rows)),
            whole((rows, 1)),
        ],
        out_specs=[
            whole((rows, width)),
            pl.BlockSpec((1, width, 3 * gw), lambda g: (g, 0, 0)),
            pl.BlockSpec((gw, width), lambda g: (g, 0)),
        ],
        out_shape=[
            jax.ShapeDtypeStruct((rows, width), jnp.bfloat16),
            jax.ShapeDtypeStruct((steps, width, 3 * gw), jnp.bfloat16),
            jax.ShapeDtypeStruct((width, width), jnp.bfloat16),
        ],
        scratch_shapes=[
            pltpu.VMEM((rows, width), jnp.bfloat16),
            pltpu.VMEM((width, rows), jnp.bfloat16),
            pltpu.VMEM((rows, rows), jnp.float32),
            pltpu.VMEM((rows, width), jnp.float32),
            pltpu.VMEM((rows, 3 * gw), jnp.bfloat16),
            pltpu.VMEM((gw, rows), jnp.bfloat16),
        ],
        compiler_params=pltpu.CompilerParams(vmem_limit_bytes=60 * 1024 * 1024),
    )(
        sharpness,
        x,
        dy,
        norm_gain[None, :],
        w_qkv,
        w_qkv,
        w_qkv,
        w_out,
        cohort_ids[:, None],
        cohort_ids[None, :],
        seen,
    )


def body(hidden_in, grad_out, norm_gain, w_qkv, w_out, sharpness, cohort_ids, observed):
    width = hidden_in.shape[-1]
    heads = sharpness.shape[0]
    x = lax.all_to_all(hidden_in, "dev", split_axis=1, concat_axis=0, tiled=True)
    dy = lax.all_to_all(grad_out, "dev", split_axis=1, concat_axis=0, tiled=True)
    campaigns, patches, _ = x.shape
    gin, gqkv, gwo = [], 0.0, 0.0
    for p in range(patches):
        a, b, c = patch_grads(
            x[:, p], dy[:, p], norm_gain, w_qkv, w_out, sharpness, cohort_ids, observed[:, p : p + 1]
        )
        gin.append(a)
        gqkv, gwo = (b, c) if p == 0 else (gqkv + b, gwo + c)
    grad_in = lax.all_to_all(
        jnp.stack(gin, axis=1), "dev", split_axis=0, concat_axis=1, tiled=True
    )
    steps = gqkv.shape[0]
    gqkv = lax.psum_scatter(gqkv, "dev", scatter_dimension=1, tiled=True)
    gwo = lax.psum_scatter(gwo, "dev", scatter_dimension=0, tiled=True)
    part = gqkv.shape[1]
    gqkv = gqkv.reshape(steps, part, 3, width // steps).transpose(1, 2, 0, 3).reshape(part, 3 * width)
    return (grad_in, gqkv.astype(jnp.float32), gwo.astype(jnp.float32))


def solution(mesh):
    in_specs = (
        P(("grp", "dev"), None, None),
        P(("grp", "dev"), None, None),
        P(),
        P(),
        P(),
        P(),
        P("grp"),
        P("grp", "dev"),
    )
    out_specs = (P(("grp", "dev"), None, None), P(("grp", "dev"), None), P(("grp", "dev"), None))
    return jax.shard_map(body, mesh=mesh, in_specs=in_specs, out_specs=out_specs, check_vma=False)
```

time: 464 us -> 350 us (0.75)
  matrix products: 149 us -> 0 us
  Pallas kernels: 0 us -> 56 us
  waiting for transfers between devices: 179 us -> 235 us
  other arithmetic: 41.2 us -> 8.81 us
  local copies, waits for them, and re-layouts: 50.9 us -> 20.2 us
  loops' own time: 7.86 us -> 0 us
    dot_general x77 -> x0, matrix products: 149 us -> none  [the longest x12 23.3 us: head_step(): jnp.einsum('pij,ipe->jpe', grad_scores, query_head, preferred_element_typ...]
    unnamed x2 -> x3, waiting for transfers between devices: 0.03 us -> 98.4 us
    reduce_scatter x2 -> x1, waiting for transfers between devices: 153 us -> 84.4 us  [body(): gwo = lax.psum_scatter(gwo, 'dev', scatter_dimension=0, tiled=True)]
    pallas_call x0 -> x1, Pallas kernels: none -> 56 us  [patch_grads(): pl.pallas_call(functools.partial(compute_kernel, head_size, group), grid=...]
    all_to_all x1, waiting for transfers between devices: 0.09 us -> 24.9 us  [body(): lax.all_to_all(grad_out, 'dev', split_axis=1, concat_axis=0, tiled=True)]
    convert_element_type x18 -> x2, other arithmetic: 18.3 us -> 1.42 us  [body(): return (grad_in, gqkv.astype(jnp.float32), gwo.astype(jnp.float32))]
    slice x5 -> x0, local copies, waits for them, and re-layouts: 11.3 us -> none  [the longest x2 5.11 us: forward_part(): key_raw = projected[:, width:2 * width].reshape(shape4)]
    another operation x1 -> x0, loops' own time: 7.86 us -> none  [body(): lax.fori_loop(0, heads, head_step, (empty, empty, empty, empty))]
  transfers between devices with their start and end apart: 5 -> 5, of which waited for: 4 -> 4; matrix products, arithmetic and copies ran while one was open for 16% -> 6% of each run, Pallas kernels for 0% -> 0%
where the time goes in v1:
time: 350 us; the launch traced here: 349 us
  waiting for transfers between devices  235 us (67%)
  Pallas kernels  56 us (16%)
  local copies, waits for them, and re-layouts  20.2 us (6%)
  starting transfers between devices  14.8 us (4%)
  between operations  14.1 us (4%)
  other arithmetic  8.81 us (3%)
    unnamed x3, waiting for transfers between devices  98.4 us
    reduce_scatter x1, waiting for transfers between devices, body(): gwo = lax.psum_scatter(gwo, 'dev', scatter_dimension=0, tiled=True)  84.4 us
    pallas_call x1, Pallas kernels, patch_grads(): pl.pallas_call(functools.partial(compute_kernel, head_size, group), grid=...  56 us
    all_to_all x1, waiting for transfers between devices, body(): lax.all_to_all(hidden_in, 'dev', split_axis=1, concat_axis=0, tiled=True)  27.4 us
    all_to_all x1, waiting for transfers between devices, body(): lax.all_to_all(grad_out, 'dev', split_axis=1, concat_axis=0, tiled=True)  24.9 us
    unnamed x18, local copies, waits for them, and re-layouts  14.3 us
    all_to_all x1, starting transfers between devices, body(): lax.all_to_all(hidden_in, 'dev', split_axis=1, concat_axis=0, tiled=True)  7.33 us
  transfers between devices with their start and end apart: 5, of which 4 were waited for; matrix products, arithmetic and copies ran while one was open for 6% of the time, Pallas kernels for 0%

profile of v1, /device:TPU:0, one launch (start us, length us, event | category | flops | bytes accessed | tf_op | source)
XLA Modules:
  0.0 349.2 jit_solution(7405848773570062063)
XLA Ops:
  7.2 2.8 copy.22
  9.9 7.3 %all-to-all-start = ((bf16[20,32,768]{2,0,1:T(8,128)(2,1)}), bf16[20,32,768]{2,0,1:T(8,128)(2,1)S(1)}, u32[]{:S(2)}, u32[]{:S(2)}) async-start(bf16[20,32,768]{2,0,1:T(8,128)(2,1)} %copy.22), calls=%async_computation | async-start | bytes 2359296 | tf_op jit(solution)/shard_map/all_to_all | solution.py:181
  17.3 1.6 copy.23
  18.9 27.4 %all-to-all-done = bf16[20,32,768]{2,0,1:T(8,128)(2,1)S(1)} async-done(((bf16[20,32,768]{2,0,1:T(8,128)(2,1)}), bf16[20,32,768]{2,0,1:T(8,128)(2,1)S(1)}, u32[]{:S(2)}, u32[]{:S(2)}) %all-to-all-start) | async-done | bytes 983072 | tf_op jit(solution)/shard_map/all_to_all | solution.py:181
  46.3 3.6 %all-to-all-start.1 = ((bf16[20,32,768]{2,0,1:T(8,128)(2,1)}), bf16[20,32,768]{2,0,1:T(8,128)(2,1)S(1)}, u32[]{:S(2)}, u32[]{:S(2)}) async-start(bf16[20,32,768]{2,0,1:T(8,128)(2,1)} %copy.23), calls=%async_computation.1 | async-start | bytes 2359296 | tf_op jit(solution)/shard_map/all_to_all | solution.py:182
  49.9 0.0 reduce-scatter.5.cloned.1.call-start
  50.0 0.6 broadcast_in_dim.11.cohort_row_ref
  50.5 0.9 broadcast_in_dim.12.cohort_col_ref
  51.4 0.6 broadcast_in_dim.9.gain_ref
  52.0 0.9 copy.25.seen_ref
  52.9 1.0 squeeze.6.x_ref
  54.0 24.9 %all-to-all-done.1 = bf16[20,32,768]{2,0,1:T(8,128)(2,1)S(1)} async-done(((bf16[20,32,768]{2,0,1:T(8,128)(2,1)}), bf16[20,32,768]{2,0,1:T(8,128)(2,1)S(1)}, u32[]{:S(2)}, u32[]{:S(2)}) %all-to-all-start.1) | async-done | bytes 983072 | tf_op jit(solution)/shard_map/all_to_all | solution.py:182
  78.9 1.0 squeeze.7.dy_ref
  80.0 56.0 %shard_map.103 = (bf16[640,768]{1,0:T(8,128)(2,1)}, bf16[6,768,384]{2,1,0:T(8,128)(2,1)}, bf16[768,768]{1,0:T(8,128)(2,1)}) custom-call(f32[12]{0:T(128)} %sharp_ref.1, bf16[640,768]{1,0:T(8,128)(2,1)} %squeeze.6.x_ref, bf16[640,768]{1,0:T(8,128)(2,1)} %squeeze.7.dy_ref, f32[1,768]{1,0:T(1,128)} %broadcast_in_dim.9.gain_ref, bf16[768,2304]{1,0:T(8,128)(2,1)} %wv_ref.1, ...), custom_call_target="tpu_custom_call" | custom-call | tf_op jit(solution)/shard_map/pallas_call | solution.py:128
  136.0 0.2 reduce-scatter.7.cloned.1.call-start
  136.3 4.2 %copy.32 = bf16[96,8,6,384]{3,1,2,0:T(8,128)(2,1)} copy(bf16[96,8,6,384]{3,1,0,2:T(8,128)(2,1)} %bitcast.24) | data formatting | bytes 7077888
  140.4 0.5 broadcast.1
  141.0 0.7 copy-done.1
  141.6 1.4 reduce.1
  143.0 1.2 reshape.19
  144.3 3.6 %all-to-all-start.2 = ((bf16[32,2,7680]{2,1,0:T(2,128)(2,1)}), bf16[32,2,7680]{2,1,0:T(2,128)(2,1)S(1)}, u32[]{:S(2)}, u32[]{:S(2)}) async-start(bf16[32,2,7680]{2,1,0:T(2,128)(2,1)} %reshape.19), calls=%async_computation.2 | async-start | bytes 1966080 | tf_op jit(solution)/shard_map/all_to_all | solution.py:191
  147.9 84.4 %reduce-scatter.5.cloned.1.call-done = bf16[24,768]{1,0:T(8,128)(2,1)} async-done(((bf16[768,768]{1,0:T(8,128)(2,1)}), bf16[24,768]{1,0:T(8,128)(2,1)}) %reduce-scatter.5.cloned.1.call-update) | async-done | bytes 36880 | tf_op jit(solution)/shard_map/reduce_scatter | solution.py:196
  232.3 1.4 convert_element_type.19
  233.7 0.8 reshape.20
  234.5 6.0 %reduce = bf16[640,768]{1,0:T(8,128)(2,1)S(1)} reduce(bf16[640,1,768]{2,1,0:T(2,128)(2,1)S(1)} %reshape.20, bf16[]{:T(256)} %constant.3), dimensions={1}, to_apply=%all_to_all.41.reduce_sub_computation | reduce | bytes 1966082 | tf_op jit(solution)/shard_map/all_to_all | solution.py:191
  240.5 0.2 all_to_all.42
  240.8 1.1 copy.28
  241.9 98.3 %reduce-scatter.7.cloned.1.call-done = bf16[24,2304]{1,0:T(8,128)(2,1)} async-done(((bf16[768,2304]{1,0:T(8,128)(2,1)}), bf16[24,2304]{1,0:T(8,128)(2,1)}) %reduce-scatter.7.cloned.1.call-update) | async-done | bytes 110608
  340.3 1.0 reshape.17
  341.3 0.1 reshape.15
  341.4 0.1 copy.27
  341.6 0.7 reshape.14
  (13 shorter events, 0.1 us)
Async XLA Ops:
  9.9 7.3 %copy-start = (bf16[20,32,768]{2,1,0:T(8,128)(2,1)S(1)}, bf16[20,32,768]{2,1,0:T(8,128)(2,1)}, u32[]{:S(2)}) copy-start(bf16[20,32,768]{2,1,0:T(8,128)(2,1)} %param.9) | copy-start | bytes 2949124
  9.9 36.3 %all-to-all-start = ((bf16[20,32,768]{2,0,1:T(8,128)(2,1)}), bf16[20,32,768]{2,0,1:T(8,128)(2,1)S(1)}, u32[]{:S(2)}, u32[]{:S(2)}) async-start(bf16[20,32,768]{2,0,1:T(8,128)(2,1)} %copy.22), calls=%async_computation | async-start | bytes 2359296 | tf_op jit(solution)/shard_map/all_to_all | solution.py:181
  18.8 31.1 %copy-start.2 = (s32[640]{0:T(1024)S(1)}, s32[640]{0:T(1024)}, u32[]{:S(2)}) copy-start(s32[640]{0:T(1024)} %param.14) | copy-start | bytes 7684
  18.8 32.6 %copy-start.3 = (f32[768]{0:T(1024)S(1)}, f32[768]{0:T(1024)}, u32[]{:S(2)}) copy-start(f32[768]{0:T(1024)} %param.10) | copy-start | bytes 9220
  18.9 33.2 %copy-start.4 = (s32[640,1]{0,1:T(1,128)S(1)}, s32[640,1]{0,1:T(1,128)}, u32[]{:S(2)}) copy-start(s32[640,1]{0,1:T(1,128)} %param.15) | copy-start | bytes 7684
  46.3 32.6 %all-to-all-start.1 = ((bf16[20,32,768]{2,0,1:T(8,128)(2,1)}), bf16[20,32,768]{2,0,1:T(8,128)(2,1)S(1)}, u32[]{:S(2)}, u32[]{:S(2)}) async-start(bf16[20,32,768]{2,0,1:T(8,128)(2,1)} %copy.23), calls=%async_computation.1 | async-start | bytes 2359296 | tf_op jit(solution)/shard_map/all_to_all | solution.py:182
  49.9 182.4 %reduce-scatter.5.cloned.1.call-start = ((), (), s32[]{:S(2)}) async-start(), calls=%async_computation.5 | async-start | bytes 1216512 | tf_op jit(solution)/shard_map/reduce_scatter | solution.py:196
  136.0 204.2 %reduce-scatter.7.cloned.1.call-start = ((), (), s32[]{:S(2)}) async-start(), calls=%async_computation.6 | async-start | bytes 3649536
  140.4 1.2 copy-start.1
  144.3 89.4 %all-to-all-start.2 = ((bf16[32,2,7680]{2,1,0:T(2,128)(2,1)}), bf16[32,2,7680]{2,1,0:T(2,128)(2,1)S(1)}, u32[]{:S(2)}, u32[]{:S(2)}) async-start(bf16[32,2,7680]{2,1,0:T(2,128)(2,1)} %reshape.19), calls=%async_computation.2 | async-start | bytes 1966080 | tf_op jit(solution)/shard_map/all_to_all | solution.py:191
Sparse Core Ops, SparseCore 0:
  136.2 96.1 reduce-scatter.4
  237.7 102.4 reduce-scatter.6

commit v2 on v1

--- a/solution.py
+++ b/solution.py
@@ -175,9 +175,120 @@
     )
 
 
-def body(hidden_in, grad_out, norm_gain, w_qkv, w_out, sharpness, cohort_ids, observed):
+def scatter_kernel(n, chunks, group_cols, qkv_ref, wo_ref, out_ref, wout_ref, *scratch):
+    bits = n.bit_length() - 1
+    recv = scratch[:bits]
+    kept = (None,) + scratch[bits : 2 * bits - 1]
+    send_sem, recv_sem = scratch[2 * bits - 1 :]
+    me = lax.axis_index("dev")
+    bit = [(me // (1 << b)) % 2 for b in range(bits)]
+    peer = [me + (1 - 2 * bit[b]) * (1 << b) for b in range(bits)]
+    groups = qkv_ref.shape[0]
+    cols = qkv_ref.shape[-1]
+    width = wout_ref.shape[-1]
+
+    barrier = pltpu.get_barrier_semaphore()
+    for b in range(bits):
+        pl.semaphore_signal(
+            barrier, inc=1, device_id={"dev": peer[b]}, device_id_type=pl.DeviceIdType.MESH
+        )
+    pl.semaphore_wait(barrier, bits)
+
+    def order_of(chunk):
+        order = list(range(bits))
+        if chunk % 2 and bits > 2:
+            order[1], order[2] = order[2], order[1]
+        return order
+
+    def source(chunk, phase, side):
+        order = order_of(chunk)
+        left = sorted(set(range(bits)) - set(order[:phase]), reverse=True)
+        picks = tuple(side if b == order[phase] else slice(None) for b in left)
+        if phase:
+            return kept[phase], (chunk,) + picks
+        if chunk < groups:
+            return qkv_ref, (chunk,) + picks
+        start = (chunk - groups) * cols
+        return wo_ref, picks + (slice(None), slice(start, start + cols))
+
+    copies = {}
+
+    def begin(chunk, phase):
+        b = order_of(chunk)[phase]
+        ref, index = source(chunk, phase, 1 - bit[b])
+        copy = pltpu.make_async_remote_copy(
+            src_ref=ref.at[index],
+            dst_ref=recv[phase].at[chunk],
+            send_sem=send_sem.at[chunk, phase],
+            recv_sem=recv_sem.at[chunk, phase],
+            device_id={"dev": peer[b]},
+            device_id_type=pl.DeviceIdType.MESH,
+        )
+        copy.start()
+        copies[chunk, phase] = copy
+
+    def finish(chunk, phase):
+        b = order_of(chunk)[phase]
+        copies[chunk, phase].wait_recv()
+        ref, index = source(chunk, phase, bit[b])
+        total = ref[index].astype(jnp.float32) + recv[phase][chunk].astype(jnp.float32)
+        if phase + 1 < bits:
+            kept[phase + 1][chunk] = total.astype(jnp.bfloat16)
+            begin(chunk, phase + 1)
+        elif chunk < groups:
+            for part in range(3):
+                at = part * width + chunk * group_cols
+                out_ref[:, at : at + group_cols] = total[
+                    :, part * group_cols : (part + 1) * group_cols
+                ]
+        else:
+            at = (chunk - groups) * cols
+            wout_ref[:, at : at + cols] = total
+
+    for chunk in range(chunks):
+        begin(chunk, 0)
+    pairs = -(-chunks // 2)
+    for wave in range(pairs + bits - 1):
+        for phase in reversed(range(bits)):
+            pair = wave - phase
+            if 0 <= pair < pairs:
+                for chunk in range(2 * pair, min(2 * pair + 2, chunks)):
+                    finish(chunk, phase)
+    for copy in copies.values():
+        copy.wait_send()
+
+
+def scatter_sums(gqkv, gwo, n):
+    groups, width, cols = gqkv.shape
+    bits = n.bit_length() - 1
+    rows = width // n
+    chunks = groups + width // cols
+    cube = (2,) * bits
+    recv = [pltpu.VMEM((chunks,) + (2,) * (bits - 1 - p) + (rows, cols), jnp.bfloat16) for p in range(bits)]
+    kept = [pltpu.VMEM((chunks,) + (2,) * (bits - p) + (rows, cols), jnp.bfloat16) for p in range(1, bits)]
+    vmem = pl.BlockSpec(memory_space=pltpu.VMEM)
+    return pl.pallas_call(
+        functools.partial(scatter_kernel, n, chunks, cols // 3),
+        in_specs=[vmem, vmem],
+        out_specs=[vmem, vmem],
+        out_shape=[
+            jax.ShapeDtypeStruct((rows, 3 * width), jnp.float32),
+            jax.ShapeDtypeStruct((rows, width), jnp.float32),
+        ],
+        scratch_shapes=recv
+        + kept
+        + [pltpu.SemaphoreType.DMA((chunks, bits)), pltpu.SemaphoreType.DMA((chunks, bits))],
+        compiler_params=pltpu.CompilerParams(
+            collective_id=0, has_side_effects=True, vmem_limit_bytes=40 * 1024 * 1024
+        ),
+        cost_estimate=pl.CostEstimate(
+            flops=40_000_000_000, bytes_accessed=8 * gqkv.size, transcendentals=0
+        ),
+    )(gqkv.reshape((groups,) + cube + (rows, cols)), gwo.reshape(cube + (rows, width)))
+
+
+def body(n, hidden_in, grad_out, norm_gain, w_qkv, w_out, sharpness, cohort_ids, observed):
     width = hidden_in.shape[-1]
-    heads = sharpness.shape[0]
     x = lax.all_to_all(hidden_in, "dev", split_axis=1, concat_axis=0, tiled=True)
     dy = lax.all_to_all(grad_out, "dev", split_axis=1, concat_axis=0, tiled=True)
     campaigns, patches, _ = x.shape
@@ -186,17 +297,12 @@
         a, b, c = patch_grads(
             x[:, p], dy[:, p], norm_gain, w_qkv, w_out, sharpness, cohort_ids, observed[:, p : p + 1]
         )
-        gin.append(a)
+        gin.append(a.reshape(n, campaigns // n, width))
         gqkv, gwo = (b, c) if p == 0 else (gqkv + b, gwo + c)
-    grad_in = lax.all_to_all(
-        jnp.stack(gin, axis=1), "dev", split_axis=0, concat_axis=1, tiled=True
-    )
-    steps = gqkv.shape[0]
-    gqkv = lax.psum_scatter(gqkv, "dev", scatter_dimension=1, tiled=True)
-    gwo = lax.psum_scatter(gwo, "dev", scatter_dimension=0, tiled=True)
-    part = gqkv.shape[1]
-    gqkv = gqkv.reshape(steps, part, 3, width // steps).transpose(1, 2, 0, 3).reshape(part, 3 * width)
-    return (grad_in, gqkv.astype(jnp.float32), gwo.astype(jnp.float32))
+    gin = gin[0] if patches == 1 else jnp.stack(gin, axis=1).reshape(n * patches, campaigns // n, width)
+    grad_in = lax.all_to_all(gin, "dev", split_axis=0, concat_axis=0, tiled=True).transpose(1, 0, 2)
+    grad_qkv, grad_wout = scatter_sums(gqkv, gwo, n)
+    return (grad_in, grad_qkv, grad_wout)
 
 
 def solution(mesh):
@@ -211,4 +317,4 @@
         P("grp", "dev"),
     )
     out_specs = (P(("grp", "dev"), None, None), P(("grp", "dev"), None), P(("grp", "dev"), None))
-    return jax.shard_map(body, mesh=mesh, in_specs=in_specs, out_specs=out_specs, check_vma=False)
+    return jax.shard_map(functools.partial(body, mesh.shape["dev"]), mesh=mesh, in_specs=in_specs, out_specs=out_specs, check_vma=False)

time: 350 us -> 186 us (0.53)
  waiting for transfers between devices: 235 us -> 52.4 us
  Pallas kernels: 56 us -> 102 us
  between operations: 14.1 us -> 0.71 us
  other arithmetic: 8.81 us -> 0 us
  local copies, waits for them, and re-layouts: 20.2 us -> 16 us
    unnamed x3 -> x0, waiting for transfers between devices: 98.4 us -> none
    reduce_scatter x1 -> x0, waiting for transfers between devices: 84.4 us -> none  [body(): gwo = lax.psum_scatter(gwo, 'dev', scatter_dimension=0, tiled=True)]
    pallas_call x0 -> x1, Pallas kernels: none -> 46 us  [scatter_sums(): pl.pallas_call(functools.partial(scatter_kernel, n, chunks, cols // 3), i...]
    all_to_all x1 -> x0, other arithmetic: 5.99 us -> none  [body(): lax.all_to_all(jnp.stack(gin, axis=1), 'dev', split_axis=0, concat_axis=1...]
    unnamed x18, local copies, waits for them, and re-layouts: 14.3 us -> 9.73 us
  transfers between devices with their start and end apart: 5 -> 3, of which waited for: 4 -> 2; matrix products, arithmetic and copies ran while one was open for 6% -> 3% of each run, Pallas kernels for 0% -> 25%
where the time goes in v2:
time: 186 us
  Pallas kernels  102 us (55%)
  waiting for transfers between devices  52.4 us (28%)
  local copies, waits for them, and re-layouts  16 us (9%)
  starting transfers between devices  14.6 us (8%)
    pallas_call x1, Pallas kernels, patch_grads(): pl.pallas_call(functools.partial(compute_kernel, head_size, group), grid=...  56 us
    pallas_call x1, Pallas kernels, scatter_sums(): pl.pallas_call(functools.partial(scatter_kernel, n, chunks, cols // 3), i...  46 us
    all_to_all x1, waiting for transfers between devices, body(): lax.all_to_all(hidden_in, 'dev', split_axis=1, concat_axis=0, tiled=True)  27.4 us
    all_to_all x1, waiting for transfers between devices, body(): lax.all_to_all(grad_out, 'dev', split_axis=1, concat_axis=0, tiled=True)  25 us
    unnamed x18, local copies, waits for them, and re-layouts  9.73 us
    all_to_all x1, starting transfers between devices, body(): lax.all_to_all(hidden_in, 'dev', split_axis=1, concat_axis=0, tiled=True)  7.33 us
  transfers between devices with their start and end apart: 3, of which 2 were waited for; matrix products, arithmetic and copies ran while one was open for 3% of the time, Pallas kernels for 25%

profile of v2, /device:TPU:0, one launch (start us, length us, event | category | flops | bytes accessed | tf_op | source)
XLA Modules:
  0.0 185.7 jit_solution(7676877089103153180)
XLA Ops:
  0.6 2.8 %copy.20 = bf16[20,32,768]{2,0,1:T(8,128)(2,1)} copy(bf16[20,32,768]{2,1,0:T(8,128)(2,1)} %param.8) | data formatting | bytes 1966080 | tf_op args[0]
  3.4 0.0 copy-start.2
  3.4 7.3 %all-to-all-start = ((bf16[20,32,768]{2,0,1:T(8,128)(2,1)}), bf16[20,32,768]{2,0,1:T(8,128)(2,1)S(1)}, u32[]{:S(2)}, u32[]{:S(2)}) async-start(bf16[20,32,768]{2,0,1:T(8,128)(2,1)} %copy.20), calls=%async_computation | async-start | bytes 2359296 | tf_op jit(solution)/shard_map/all_to_all | solution.py:292
  10.7 0.0 copy-done.2
  10.7 1.6 copy.21
  12.3 0.0 copy-start.3
  12.3 0.0 copy-start.4
  12.3 0.0 copy-start.5
  12.3 27.4 %all-to-all-done = bf16[20,32,768]{2,0,1:T(8,128)(2,1)S(1)} async-done(((bf16[20,32,768]{2,0,1:T(8,128)(2,1)}), bf16[20,32,768]{2,0,1:T(8,128)(2,1)S(1)}, u32[]{:S(2)}, u32[]{:S(2)}) %all-to-all-start) | async-done | bytes 983072 | tf_op jit(solution)/shard_map/all_to_all | solution.py:292
  39.7 3.6 %all-to-all-start.1 = ((bf16[20,32,768]{2,0,1:T(8,128)(2,1)}), bf16[20,32,768]{2,0,1:T(8,128)(2,1)S(1)}, u32[]{:S(2)}, u32[]{:S(2)}) async-start(bf16[20,32,768]{2,0,1:T(8,128)(2,1)} %copy.21), calls=%async_computation.1 | async-start | bytes 2359296 | tf_op jit(solution)/shard_map/all_to_all | solution.py:293
  43.4 0.0 copy-done.3
  43.4 0.6 broadcast_in_dim.11.cohort_row_ref
  44.0 0.9 broadcast_in_dim.12.cohort_col_ref
  44.9 0.0 copy-done.4
  44.9 0.6 broadcast_in_dim.9.gain_ref
  45.4 0.0 copy-done.5
  45.4 0.9 copy.23.seen_ref
  46.4 1.0 squeeze.6.x_ref
  47.4 25.0 %all-to-all-done.1 = bf16[20,32,768]{2,0,1:T(8,128)(2,1)S(1)} async-done(((bf16[20,32,768]{2,0,1:T(8,128)(2,1)}), bf16[20,32,768]{2,0,1:T(8,128)(2,1)S(1)}, u32[]{:S(2)}, u32[]{:S(2)}) %all-to-all-start.1) | async-done | bytes 983072 | tf_op jit(solution)/shard_map/all_to_all | solution.py:293
  72.4 1.1 squeeze.7.dy_ref
  73.5 56.0 %shard_map.103 = (bf16[640,768]{1,0:T(8,128)(2,1)}, bf16[6,768,384]{2,1,0:T(8,128)(2,1)}, bf16[768,768]{1,0:T(8,128)(2,1)}) custom-call(f32[12]{0:T(128)} %sharp_ref.1, bf16[640,768]{1,0:T(8,128)(2,1)} %squeeze.6.x_ref, bf16[640,768]{1,0:T(8,128)(2,1)} %squeeze.7.dy_ref, f32[1,768]{1,0:T(1,128)} %broadcast_in_dim.9.gain_ref, bf16[768,2304]{1,0:T(8,128)(2,1)} %wv_ref.1, ...), custom_call_target="tpu_custom_call" | custom-call | tf_op jit(solution)/shard_map/pallas_call | solution.py:128
  129.5 2.1 %reshape.17 = bf16[32,20,768]{2,1,0:T(8,128)(2,1)} reshape(bf16[640,768]{1,0:T(8,128)(2,1)} %get-tuple-element.8) | data formatting | bytes 1966080 | tf_op jit(solution)/shard_map/reshape | solution.py:300
  131.6 0.0 copy-start.1
  131.6 3.6 %all-to-all-start.2 = ((bf16[32,20,768]{2,1,0:T(8,128)(2,1)}), bf16[32,20,768]{2,1,0:T(8,128)(2,1)S(1)}, u32[]{:S(2)}, u32[]{:S(2)}) async-start(bf16[32,20,768]{2,1,0:T(8,128)(2,1)} %reshape.17), calls=%async_computation.2 | async-start | bytes 2359296 | tf_op jit(solution)/shard_map/all_to_all | solution.py:303
  135.2 0.0 copy-done.1
  135.3 0.0 copy-start
  135.3 2.0 %copy-done = bf16[6,768,384]{2,1,0:T(8,128)(2,1)S(1)} copy-done((bf16[6,768,384]{2,1,0:T(8,128)(2,1)S(1)}, bf16[6,768,384]{2,1,0:T(8,128)(2,1)}, u32[]{:S(2)}) %copy-start) | copy-done | bytes 3538968
  137.3 46.0 %shard_map.104 = (f32[24,2304]{1,0:T(8,128)S(1)}, f32[24,768]{1,0:T(8,128)S(1)}) custom-call(bf16[6,2,2,2,2,2,24,384]{7,6,5,4,3,2,1,0:T(8,128)(2,1)S(1)} %bitcast.13, bf16[2,2,2,2,2,24,768]{6,5,4,3,2,1,0:T(8,128)(2,1)S(1)} %bitcast.14), custom_call_target="tpu_custom_call" | custom-call | flops 40000000000 | bytes 14155776 | tf_op jit(solution)/shard_map/pallas_call | solution.py:270
  183.3 0.0 all-to-all-done.2
  183.3 1.1 copy.24
  184.4 0.7 copy.27
  185.1 0.6 copy.28
Async XLA Ops:
  3.4 7.3 %copy-start.2 = (bf16[20,32,768]{2,1,0:T(8,128)(2,1)S(1)}, bf16[20,32,768]{2,1,0:T(8,128)(2,1)}, u32[]{:S(2)}) copy-start(bf16[20,32,768]{2,1,0:T(8,128)(2,1)} %param.9) | copy-start | bytes 2949124
  3.4 36.3 %all-to-all-start = ((bf16[20,32,768]{2,0,1:T(8,128)(2,1)}), bf16[20,32,768]{2,0,1:T(8,128)(2,1)S(1)}, u32[]{:S(2)}, u32[]{:S(2)}) async-start(bf16[20,32,768]{2,0,1:T(8,128)(2,1)} %copy.20), calls=%async_computation | async-start | bytes 2359296 | tf_op jit(solution)/shard_map/all_to_all | solution.py:292
  12.3 31.1 %copy-start.3 = (s32[640]{0:T(1024)S(1)}, s32[640]{0:T(1024)}, u32[]{:S(2)}) copy-start(s32[640]{0:T(1024)} %param.14) | copy-start | bytes 7684
  12.3 32.5 %copy-start.4 = (f32[768]{0:T(1024)S(1)}, f32[768]{0:T(1024)}, u32[]{:S(2)}) copy-start(f32[768]{0:T(1024)} %param.10) | copy-start | bytes 9220
  12.3 33.1 %copy-start.5 = (s32[640,1]{0,1:T(1,128)S(1)}, s32[640,1]{0,1:T(1,128)}, u32[]{:S(2)}) copy-start(s32[640,1]{0,1:T(1,128)} %param.15) | copy-start | bytes 7684
  39.7 32.6 %all-to-all-start.1 = ((bf16[20,32,768]{2,0,1:T(8,128)(2,1)}), bf16[20,32,768]{2,0,1:T(8,128)(2,1)S(1)}, u32[]{:S(2)}, u32[]{:S(2)}) async-start(bf16[20,32,768]{2,0,1:T(8,128)(2,1)} %copy.21), calls=%async_computation.1 | async-start | bytes 2359296 | tf_op jit(solution)/shard_map/all_to_all | solution.py:293
  131.6 3.6 %copy-start.1 = (bf16[768,768]{1,0:T(8,128)(2,1)S(1)}, bf16[768,768]{1,0:T(8,128)(2,1)}, u32[]{:S(2)}) copy-start(bf16[768,768]{1,0:T(8,128)(2,1)} %get-tuple-element.10) | copy-start | bytes 3538948
  131.6 51.6 %all-to-all-start.2 = ((bf16[32,20,768]{2,1,0:T(8,128)(2,1)}), bf16[32,20,768]{2,1,0:T(8,128)(2,1)S(1)}, u32[]{:S(2)}, u32[]{:S(2)}) async-start(bf16[32,20,768]{2,1,0:T(8,128)(2,1)} %reshape.17), calls=%async_computation.2 | async-start | bytes 2359296 | tf_op jit(solution)/shard_map/all_to_all | solution.py:303
  135.3 2.0 %copy-start = (bf16[6,768,384]{2,1,0:T(8,128)(2,1)S(1)}, bf16[6,768,384]{2,1,0:T(8,128)(2,1)}, u32[]{:S(2)}) copy-start(bf16[6,768,384]{2,1,0:T(8,128)(2,1)} %get-tuple-element.9) | copy-start | bytes 10616836

commit v3 on v2

--- a/solution.py
+++ b/solution.py
@@ -8,6 +8,7 @@
 from jax.experimental.pallas import tpu as pltpu
 from jax.sharding import PartitionSpec as P
 
+
 epsilon = 1e-06
 log2e = math.log2(math.e)
 
@@ -16,33 +17,30 @@
     return lax.dot_general(left, right, ((dims[0], dims[1]), ((), ())), preferred_element_type=jnp.float32)
 
 
-def compute_kernel(
+def forward_kernel(
     head_size,
     group,
     sharp_ref,
     x_ref,
-    dy_ref,
     gain_ref,
     wq_ref,
     wk_ref,
     wv_ref,
-    wo_ref,
     cohort_col_ref,
     cohort_row_ref,
     seen_ref,
-    gin_ref,
-    gqkv_ref,
-    gwo_ref,
+    normed_t_ref,
+    q_ref,
+    k_ref,
+    v_ref,
+    inv_ref,
+    probs_ref,
+    att_ref,
     normed_ref,
-    normed_t_ref,
     mask_ref,
-    acc_ref,
-    dproj_ref,
-    att_ref,
 ):
     step = pl.program_id(0)
-    rows, width = x_ref.shape
-    gw = group * head_size
+    rows, _ = x_ref.shape
 
     @pl.when(step == 0)
     def _():
@@ -57,34 +55,73 @@
         )
         seen = jnp.broadcast_to(seen_ref[...], (rows, rows)) == 1
         mask_ref[...] = jnp.where(same & (seen | diagonal), 1.0, 0.0)
-        acc_ref[...] = jnp.zeros_like(acc_ref)
 
     normed = normed_ref[...]
     q_raw = dot(normed, wq_ref[...], ((1,), (0,)))
     k_raw = dot(normed, wk_ref[...], ((1,), (0,)))
-    v_half = dot(normed, wv_ref[...], ((1,), (0,))).astype(jnp.bfloat16)
-    da_half = dot(dy_ref[...], wo_ref[...], ((1,), (1,))).astype(jnp.bfloat16)
+    v_raw = dot(normed, wv_ref[...], ((1,), (0,)))
+    v_ref[...] = v_raw.astype(jnp.bfloat16)
     for h in range(group):
-        lanes = slice(h * head_size, (h + 1) * head_size)
+        base = h * head_size
+        lanes = slice(base, base + head_size)
         q = q_raw[:, lanes]
         k = k_raw[:, lanes]
-        v = v_half[:, lanes]
-        da = da_half[:, lanes]
+        v_t = v_raw[:, lanes].T.astype(jnp.bfloat16)
         q_inv = lax.rsqrt(jnp.mean(q * q, axis=-1, keepdims=True) + epsilon)
         k_inv = lax.rsqrt(jnp.mean(k * k, axis=-1, keepdims=True) + epsilon)
-        q_unit = q * q_inv
-        k_unit = k * k_inv
-        q_half = q_unit.astype(jnp.bfloat16)
-        k_half = k_unit.astype(jnp.bfloat16)
-        k_t = k_unit.T.astype(jnp.bfloat16)
-        v_t = v.astype(jnp.float32).T.astype(jnp.bfloat16)
+        q_half = (q * q_inv).astype(jnp.bfloat16)
+        k_half = (k * k_inv).astype(jnp.bfloat16)
+        q_ref[:, lanes] = q_half
+        k_ref[:, lanes] = k_half
+        inv_ref[0, :, h : h + 1] = q_inv
+        inv_ref[0, :, group + h : group + h + 1] = k_inv
         scale = sharp_ref[step * group + h] / head_size
         scores = dot(k_half, q_half, ((1,), (1,)))
-        grad_probs = dot(v, da, ((1,), (1,)))
         weights = jnp.exp2(scores * (scale * log2e)) * mask_ref[...]
         probs = weights * (1.0 / jnp.sum(weights, axis=0, keepdims=True))
         probs_half = probs.astype(jnp.bfloat16)
-        att_t = dot(v_t, probs_half, ((1,), (0,)))
+        probs_ref[h] = probs_half
+        att_ref[base : base + head_size, :] = dot(v_t, probs_half, ((1,), (0,))).astype(jnp.bfloat16)
+
+
+def backward_kernel(
+    head_size,
+    group,
+    sharp_ref,
+    x_ref,
+    dy_ref,
+    gain_ref,
+    wq_ref,
+    wk_ref,
+    wv_ref,
+    wo_ref,
+    q_ref,
+    k_ref,
+    v_ref,
+    inv_ref,
+    probs_ref,
+    gin_ref,
+    dproj_ref,
+    acc_ref,
+):
+    step = pl.program_id(0)
+    gw = group * head_size
+    da_half = dot(dy_ref[...], wo_ref[...], ((1,), (1,))).astype(jnp.bfloat16)
+    for h in range(group):
+        base = h * head_size
+        lanes = slice(base, base + head_size)
+        q_half = q_ref[:, lanes]
+        k_half = k_ref[:, lanes]
+        q_unit = q_half.astype(jnp.float32)
+        k_unit = k_half.astype(jnp.float32)
+        da = da_half[:, lanes]
+        k_t = k_unit.T.astype(jnp.bfloat16)
+        q_inv = inv_ref[0, :, h : h + 1]
+        k_inv = inv_ref[0, :, group + h : group + h + 1]
+        scale = sharp_ref[step * group + h] / head_size
+        grad_probs = dot(v_ref[:, lanes], da, ((1,), (1,)))
+        probs_half = probs_ref[h]
+        probs = probs_half.astype(jnp.float32)
         grad_v = dot(probs_half, da, ((1,), (0,)))
         row_dot = jnp.sum(grad_probs * probs, axis=0, keepdims=True)
         grad_scores = (probs * (grad_probs - row_dot)).astype(jnp.bfloat16)
@@ -92,18 +129,22 @@
         dk = dot(grad_scores, q_half, ((1,), (0,))) * scale
         dq = q_inv * (dq - q_unit * jnp.mean(dq * q_unit, axis=-1, keepdims=True))
         dk = k_inv * (dk - k_unit * jnp.mean(dk * k_unit, axis=-1, keepdims=True))
-        base = h * head_size
         dproj_ref[:, base : base + head_size] = dq.astype(jnp.bfloat16)
         dproj_ref[:, gw + base : gw + base + head_size] = dk.astype(jnp.bfloat16)
         dproj_ref[:, 2 * gw + base : 2 * gw + base + head_size] = grad_v.astype(jnp.bfloat16)
-        att_ref[base : base + head_size, :] = att_t.astype(jnp.bfloat16)
-    gwo_ref[...] = dot(att_ref[...], dy_ref[...], ((1,), (0,))).astype(jnp.bfloat16)
-    gqkv_ref[0] = dot(normed_t_ref[...], dproj_ref[...], ((1,), (0,))).astype(jnp.bfloat16)
-    acc_ref[...] += (
+    term = (
         dot(dproj_ref[:, :gw], wq_ref[...], ((1,), (1,)))
         + dot(dproj_ref[:, gw : 2 * gw], wk_ref[...], ((1,), (1,)))
         + dot(dproj_ref[:, 2 * gw :], wv_ref[...], ((1,), (1,)))
     )
+
+    @pl.when(step == 0)
+    def _():
+        acc_ref[...] = term
+
+    @pl.when(step > 0)
+    def _():
+        acc_ref[...] += term
 
     @pl.when(step == pl.num_programs(0) - 1)
     def _():
@@ -117,6 +158,11 @@
         gin_ref[...] = result.astype(jnp.bfloat16)
 
 
+def weights_kernel(normed_t_ref, att_ref, dproj_ref, dy_ref, gqkv_ref, gwo_ref):
+    gqkv_ref[0] = dot(normed_t_ref[...], dproj_ref[...], ((1,), (0,))).astype(jnp.bfloat16)
+    gwo_ref[...] = dot(att_ref[...], dy_ref[...], ((1,), (0,))).astype(jnp.bfloat16)
+
+
 def patch_grads(x, dy, norm_gain, w_qkv, w_out, sharpness, cohort_ids, seen):
     rows, width = x.shape
     heads = sharpness.shape[0]
@@ -124,55 +170,85 @@
     group = math.gcd(heads, 2)
     steps = heads // group
     gw = group * head_size
+    half = jnp.bfloat16
     whole = lambda shape: pl.BlockSpec(shape, lambda g: (0,) * len(shape))
-    return pl.pallas_call(
-        functools.partial(compute_kernel, head_size, group),
+    cols = lambda n: pl.BlockSpec((rows, n), lambda g: (0, g))
+    lines = lambda n: pl.BlockSpec((gw, n), lambda g: (g, 0))
+    smem = pl.BlockSpec(memory_space=pltpu.SMEM)
+    weights = [
+        pl.BlockSpec((width, gw), lambda g: (0, g)),
+        pl.BlockSpec((width, gw), lambda g: (0, steps + g)),
+        pl.BlockSpec((width, gw), lambda g: (0, 2 * steps + g)),
+    ]
+    invs = pl.BlockSpec((1, rows, 2 * group), lambda g: (g, 0, 0))
+    probs_spec = pl.BlockSpec((group, rows, rows), lambda g: (g, 0, 0))
+    params = pltpu.CompilerParams(vmem_limit_bytes=60 * 1024 * 1024)
+
+    def cost(flops):
+        return pl.CostEstimate(flops=flops, bytes_accessed=rows * width * 20, transcendentals=0)
+
+    forward = pl.pallas_call(
+        functools.partial(forward_kernel, head_size, group),
         grid=(steps,),
-        in_specs=[
-            pl.BlockSpec(memory_space=pltpu.SMEM),
-            whole((rows, width)),
-            whole((rows, width)),
-            whole((1, width)),
-            pl.BlockSpec((width, gw), lambda g: (0, g)),
-            pl.BlockSpec((width, gw), lambda g: (0, steps + g)),
-            pl.BlockSpec((width, gw), lambda g: (0, 2 * steps + g)),
-            pl.BlockSpec((gw, width), lambda g: (g, 0)),
-            whole((rows, 1)),
-            whole((1, rows)),
-            whole((rows, 1)),
-        ],
-        out_specs=[
-            whole((rows, width)),
-            pl.BlockSpec((1, width, 3 * gw), lambda g: (g, 0, 0)),
-            pl.BlockSpec((gw, width), lambda g: (g, 0)),
-        ],
+        in_specs=[smem, whole((rows, width)), whole((1, width))]
+        + weights
+        + [whole((rows, 1)), whole((1, rows)), whole((rows, 1))],
+        out_specs=[whole((width, rows)), cols(gw), cols(gw), cols(gw), invs, probs_spec, lines(rows)],
         out_shape=[
-            jax.ShapeDtypeStruct((rows, width), jnp.bfloat16),
-            jax.ShapeDtypeStruct((steps, width, 3 * gw), jnp.bfloat16),
-            jax.ShapeDtypeStruct((width, width), jnp.bfloat16),
+            jax.ShapeDtypeStruct((width, rows), half),
+            jax.ShapeDtypeStruct((rows, width), half),
+            jax.ShapeDtypeStruct((rows, width), half),
+            jax.ShapeDtypeStruct((rows, width), half),
+            jax.ShapeDtypeStruct((steps, rows, 2 * group), jnp.float32),
+            jax.ShapeDtypeStruct((heads, rows, rows), half),
+            jax.ShapeDtypeStruct((width, rows), half),
         ],
         scratch_shapes=[
-            pltpu.VMEM((rows, width), jnp.bfloat16),
-            pltpu.VMEM((width, rows), jnp.bfloat16),
+            pltpu.VMEM((rows, width), half),
             pltpu.VMEM((rows, rows), jnp.float32),
-            pltpu.VMEM((rows, width), jnp.float32),
-            pltpu.VMEM((rows, 3 * gw), jnp.bfloat16),
-            pltpu.VMEM((gw, rows), jnp.bfloat16),
         ],
-        compiler_params=pltpu.CompilerParams(vmem_limit_bytes=60 * 1024 * 1024),
-    )(
+        compiler_params=params,
+        cost_estimate=cost(40_000_000_000),
+    )
+    normed_t, q, k, v, inv, probs, att = forward(
         sharpness,
         x,
-        dy,
         norm_gain[None, :],
         w_qkv,
         w_qkv,
         w_qkv,
-        w_out,
         cohort_ids[:, None],
         cohort_ids[None, :],
         seen,
     )
+    gin, dproj = pl.pallas_call(
+        functools.partial(backward_kernel, head_size, group),
+        grid=(steps,),
+        in_specs=[smem, whole((rows, width)), whole((rows, width)), whole((1, width))]
+        + weights
+        + [lines(width), cols(gw), cols(gw), cols(gw), invs, probs_spec],
+        out_specs=[whole((rows, width)), cols(3 * gw)],
+        out_shape=[
+            jax.ShapeDtypeStruct((rows, width), half),
+            jax.ShapeDtypeStruct((rows, 3 * width), half),
+        ],
+        scratch_shapes=[pltpu.VMEM((rows, width), jnp.float32)],
+        compiler_params=params,
+        cost_estimate=cost(25_000_000_000),
+    )(sharpness, x, dy, norm_gain[None, :], w_qkv, w_qkv, w_qkv, w_out, q, k, v, inv, probs)
+    gqkv, gwo = pl.pallas_call(
+        weights_kernel,
+        grid=(steps,),
+        in_specs=[whole((width, rows)), lines(rows), cols(3 * gw), whole((rows, width))],
+        out_specs=[pl.BlockSpec((1, width, 3 * gw), lambda g: (g, 0, 0)), lines(width)],
+        out_shape=[
+            jax.ShapeDtypeStruct((steps, width, 3 * gw), half),
+            jax.ShapeDtypeStruct((width, width), half),
+        ],
+        compiler_params=params,
+        cost_estimate=cost(8_000_000_000),
+    )(normed_t, att, dproj, dy)
+    return gin, gqkv, gwo
 
 
 def scatter_kernel(n, chunks, group_cols, qkv_ref, wo_ref, out_ref, wout_ref, *scratch):
@@ -287,7 +363,11 @@
     )(gqkv.reshape((groups,) + cube + (rows, cols)), gwo.reshape(cube + (rows, width)))
 
 
-def body(n, hidden_in, grad_out, norm_gain, w_qkv, w_out, sharpness, cohort_ids, observed):
+def body(n, *args):
+    return layer(n, *args)
+
+
+def layer(n, hidden_in, grad_out, norm_gain, w_qkv, w_out, sharpness, cohort_ids, observed):
     width = hidden_in.shape[-1]
     x = lax.all_to_all(hidden_in, "dev", split_axis=1, concat_axis=0, tiled=True)
     dy = lax.all_to_all(grad_out, "dev", split_axis=1, concat_axis=0, tiled=True)

time: 186 us -> 206 us (1.11)
  Pallas kernels: 102 us -> 120 us
    pallas_call x1 -> x3, Pallas kernels: 56 us -> 77.6 us  [the longest x1 43.3 us: patch_grads(): pl.pallas_call(functools.partial(backward_kernel, head_size, group), grid...]
    pallas_call x1, Pallas kernels: 46 us -> 42.4 us  [scatter_sums(): pl.pallas_call(functools.partial(scatter_kernel, n, chunks, cols // 3), i...]
where the time goes in v3:
time: 206 us; the launch traced here: 205 us
  Pallas kernels  120 us (58%)
  waiting for transfers between devices  52.4 us (25%)
  local copies, waits for them, and re-layouts  17.3 us (8%)
  starting transfers between devices  14.8 us (7%)
    pallas_call x1, Pallas kernels, patch_grads(): pl.pallas_call(functools.partial(backward_kernel, head_size, group), grid...  43.3 us
    pallas_call x1, Pallas kernels, scatter_sums(): pl.pallas_call(functools.partial(scatter_kernel, n, chunks, cols // 3), i...  42.4 us
    all_to_all x1, waiting for transfers between devices, layer(): lax.all_to_all(hidden_in, 'dev', split_axis=1, concat_axis=0, tiled=True)  27.4 us
    pallas_call x1, Pallas kernels, patch_grads(): forward(sharpness, x, norm_gain[None, :], w_qkv, w_qkv, w_qkv, cohort_ids...  25.6 us
    all_to_all x1, waiting for transfers between devices, layer(): lax.all_to_all(grad_out, 'dev', split_axis=1, concat_axis=0, tiled=True)  25 us
    unnamed x18, local copies, waits for them, and re-layouts  11 us
    pallas_call x1, Pallas kernels, patch_grads(): pl.pallas_call(weights_kernel, grid=(steps,), in_specs=[whole((width, row...  8.76 us
    all_to_all x1, starting transfers between devices, layer(): lax.all_to_all(hidden_in, 'dev', split_axis=1, concat_axis=0, tiled=True)  7.33 us
  transfers between devices with their start and end apart: 3, of which 2 were waited for; matrix products, arithmetic and copies ran while one was open for 3% of the time, Pallas kernels for 25%

profile of v3, /device:TPU:0, one launch (start us, length us, event | category | flops | bytes accessed | tf_op | source)
XLA Modules:
  0.0 205.1 jit_solution(12722185257151225699)
XLA Ops:
  0.6 2.8 %copy.20 = bf16[20,32,768]{2,0,1:T(8,128)(2,1)} copy(bf16[20,32,768]{2,1,0:T(8,128)(2,1)} %param.8) | data formatting | bytes 1966080 | tf_op args[0]
  3.4 0.0 copy-start.2
  3.4 7.3 %all-to-all-start = ((bf16[20,32,768]{2,0,1:T(8,128)(2,1)}), bf16[20,32,768]{2,0,1:T(8,128)(2,1)S(1)}, u32[]{:S(2)}, u32[]{:S(2)}) async-start(bf16[20,32,768]{2,0,1:T(8,128)(2,1)} %copy.20), calls=%async_computation | async-start | bytes 2359296 | tf_op jit(solution)/shard_map/all_to_all | solution.py:372
  10.7 0.0 copy-done.2
  10.7 1.6 copy.21
  12.3 0.0 copy-start.3
  12.3 0.0 copy-start.4
  12.3 0.0 copy-start.5
  12.3 27.4 %all-to-all-done = bf16[20,32,768]{2,0,1:T(8,128)(2,1)S(1)} async-done(((bf16[20,32,768]{2,0,1:T(8,128)(2,1)}), bf16[20,32,768]{2,0,1:T(8,128)(2,1)S(1)}, u32[]{:S(2)}, u32[]{:S(2)}) %all-to-all-start) | async-done | bytes 983072 | tf_op jit(solution)/shard_map/all_to_all | solution.py:372
  39.7 3.6 %all-to-all-start.1 = ((bf16[20,32,768]{2,0,1:T(8,128)(2,1)}), bf16[20,32,768]{2,0,1:T(8,128)(2,1)S(1)}, u32[]{:S(2)}, u32[]{:S(2)}) async-start(bf16[20,32,768]{2,0,1:T(8,128)(2,1)} %copy.21), calls=%async_computation.1 | async-start | bytes 2359296 | tf_op jit(solution)/shard_map/all_to_all | solution.py:373
  43.4 0.0 copy-done.3
  43.4 0.6 broadcast_in_dim.12.cohort_row_ref
  44.0 0.9 broadcast_in_dim.13.cohort_col_ref
  44.8 0.0 copy-done.4
  44.8 0.6 broadcast_in_dim.10.gain_ref
  45.4 0.0 copy-done.5
  45.4 0.9 copy.23.seen_ref
  46.4 1.0 squeeze.6.x_ref
  47.4 25.0 %all-to-all-done.1 = bf16[20,32,768]{2,0,1:T(8,128)(2,1)S(1)} async-done(((bf16[20,32,768]{2,0,1:T(8,128)(2,1)}), bf16[20,32,768]{2,0,1:T(8,128)(2,1)S(1)}, u32[]{:S(2)}, u32[]{:S(2)}) %all-to-all-start.1) | async-done | bytes 983072 | tf_op jit(solution)/shard_map/all_to_all | solution.py:373
  72.4 1.1 squeeze.7.dy_ref
  73.5 25.6 %shard_map.103 = (bf16[768,640]{1,0:T(8,128)(2,1)}, bf16[640,768]{1,0:T(8,128)(2,1)}, bf16[640,768]{1,0:T(8,128)(2,1)}, bf16[640,768]{1,0:T(8,128)(2,1)}, f32[6,...) custom-call(f32[12]{0:T(128)} %sharp_ref.3, bf16[640,768]{1,0:T(8,128)(2,1)} %squeeze.6.x_ref, ...), custom_call_target="tpu_custom_call" | custom-call | flops 40000000000 | bytes 9830400 | tf_op jit(solution)/shard_map/pallas_call | solution.py:213
  99.0 43.3 %shard_map.104 = (bf16[640,768]{1,0:T(8,128)(2,1)}, bf16[640,2304]{1,0:T(8,128)(2,1)}) custom-call(f32[12]{0:T(128)} %sharp_ref.3, bf16[640,768]{1,0:T(8,128)(2,1)} %squeeze.6.x_ref, bf16[640,768]{1,0:T(8,128)(2,1)} %squeeze.7.dy_ref, f32[1,768]{1,0:T(1,128)} %broadcast_in_dim.10.gain_ref, bf16[768,2304]{1,0:T(8,128)(2,1)} %wv_ref.3, ...), custom_call_target="tpu_custom_call" | custom-call | flops 24999999488 | bytes 9830400 | tf_op jit(solution)/shard_map/pallas_call | solution.py:224
  142.3 2.2 %reshape.17 = bf16[32,20,768]{2,1,0:T(8,128)(2,1)} reshape(bf16[640,768]{1,0:T(8,128)(2,1)} %get-tuple-element.21) | data formatting | bytes 1966080 | tf_op jit(solution)/shard_map/reshape | solution.py:380
  144.4 3.8 %all-to-all-start.2 = ((bf16[32,20,768]{2,1,0:T(8,128)(2,1)}), bf16[32,20,768]{2,1,0:T(8,128)(2,1)S(1)}, u32[]{:S(2)}, u32[]{:S(2)}) async-start(bf16[32,20,768]{2,1,0:T(8,128)(2,1)} %reshape.17), calls=%async_computation.2 | async-start | bytes 2359296 | tf_op jit(solution)/shard_map/all_to_all | solution.py:383
  148.2 8.8 %shard_map.105 = (bf16[6,768,384]{2,1,0:T(8,128)(2,1)}, bf16[768,768]{1,0:T(8,128)(2,1)}) custom-call(bf16[768,640]{1,0:T(8,128)(2,1)} %get-tuple-element.22.normed_t_ref, bf16[768,640]{1,0:T(8,128)(2,1)} %get-tuple-element.23.att_ref, bf16[640,2304]{1,0:T(8,128)(2,1)} %get-tuple-element.24.dproj_ref, bf16[640,768]{1,0:T(8,128)(2,1)} %squeeze.7.dy_ref), custom_call_target="tpu_custom_call" | custom-call | flops 8000000000 | bytes 9830400 | tf_op jit(solution)/shard_map/pallas_call | solution.py:239
  157.0 2.0 copy-done
  159.0 1.3 copy-done.1
  160.3 42.4 %shard_map.106 = (f32[24,2304]{1,0:T(8,128)S(1)}, f32[24,768]{1,0:T(8,128)S(1)}) custom-call(bf16[6,2,2,2,2,2,24,384]{7,6,5,4,3,2,1,0:T(8,128)(2,1)S(1)} %bitcast.13, bf16[2,2,2,2,2,24,768]{6,5,4,3,2,1,0:T(8,128)(2,1)S(1)} %bitcast.14), custom_call_target="tpu_custom_call" | custom-call | flops 40000000000 | bytes 14155776 | tf_op jit(solution)/shard_map/pallas_call | solution.py:346
  202.6 0.0 all-to-all-done.2
  202.7 1.1 copy.24
  203.8 0.7 copy.27
  204.5 0.6 copy.28
  (2 shorter events, 0.0 us)
Async XLA Ops:
  3.4 7.3 %copy-start.2 = (bf16[20,32,768]{2,1,0:T(8,128)(2,1)S(1)}, bf16[20,32,768]{2,1,0:T(8,128)(2,1)}, u32[]{:S(2)}) copy-start(bf16[20,32,768]{2,1,0:T(8,128)(2,1)} %param.9) | copy-start | bytes 2949124
  3.4 36.3 %all-to-all-start = ((bf16[20,32,768]{2,0,1:T(8,128)(2,1)}), bf16[20,32,768]{2,0,1:T(8,128)(2,1)S(1)}, u32[]{:S(2)}, u32[]{:S(2)}) async-start(bf16[20,32,768]{2,0,1:T(8,128)(2,1)} %copy.20), calls=%async_computation | async-start | bytes 2359296 | tf_op jit(solution)/shard_map/all_to_all | solution.py:372
  12.3 31.1 %copy-start.3 = (s32[640]{0:T(1024)S(1)}, s32[640]{0:T(1024)}, u32[]{:S(2)}) copy-start(s32[640]{0:T(1024)} %param.14) | copy-start | bytes 7684
  12.3 32.5 %copy-start.4 = (f32[768]{0:T(1024)S(1)}, f32[768]{0:T(1024)}, u32[]{:S(2)}) copy-start(f32[768]{0:T(1024)} %param.10) | copy-start | bytes 9220
  12.3 33.1 %copy-start.5 = (s32[640,1]{0,1:T(1,128)S(1)}, s32[640,1]{0,1:T(1,128)}, u32[]{:S(2)}) copy-start(s32[640,1]{0,1:T(1,128)} %param.15) | copy-start | bytes 7684
  39.7 32.6 %all-to-all-start.1 = ((bf16[20,32,768]{2,0,1:T(8,128)(2,1)}), bf16[20,32,768]{2,0,1:T(8,128)(2,1)S(1)}, u32[]{:S(2)}, u32[]{:S(2)}) async-start(bf16[20,32,768]{2,0,1:T(8,128)(2,1)} %copy.21), calls=%async_computation.1 | async-start | bytes 2359296 | tf_op jit(solution)/shard_map/all_to_all | solution.py:373
  144.4 58.2 %all-to-all-start.2 = ((bf16[32,20,768]{2,1,0:T(8,128)(2,1)}), bf16[32,20,768]{2,1,0:T(8,128)(2,1)S(1)}, u32[]{:S(2)}, u32[]{:S(2)}) async-start(bf16[32,20,768]{2,1,0:T(8,128)(2,1)} %reshape.17), calls=%async_computation.2 | async-start | bytes 2359296 | tf_op jit(solution)/shard_map/all_to_all | solution.py:383
  157.0 2.0 copy-start
  159.0 1.3 copy-start.1

commit v4 on v3

--- a/solution.py
+++ b/solution.py
@@ -32,6 +32,7 @@
     normed_t_ref,
     q_ref,
     k_ref,
+    k_t_ref,
     v_ref,
     inv_ref,
     probs_ref,
@@ -70,7 +71,9 @@
         q_inv = lax.rsqrt(jnp.mean(q * q, axis=-1, keepdims=True) + epsilon)
         k_inv = lax.rsqrt(jnp.mean(k * k, axis=-1, keepdims=True) + epsilon)
         q_half = (q * q_inv).astype(jnp.bfloat16)
-        k_half = (k * k_inv).astype(jnp.bfloat16)
+        k_unit = k * k_inv
+        k_half = k_unit.astype(jnp.bfloat16)
+        k_t_ref[lanes, :] = k_unit.T.astype(jnp.bfloat16)
         q_ref[:, lanes] = q_half
         k_ref[:, lanes] = k_half
         inv_ref[0, :, h : h + 1] = q_inv
@@ -91,31 +94,29 @@
     x_ref,
     dy_ref,
     gain_ref,
-    wq_ref,
-    wk_ref,
-    wv_ref,
-    wo_ref,
+    wqkv_t_ref,
+    wo_t_ref,
     q_ref,
     k_ref,
+    k_t_ref,
     v_ref,
     inv_ref,
     probs_ref,
     gin_ref,
     dproj_ref,
-    acc_ref,
 ):
     step = pl.program_id(0)
     gw = group * head_size
-    da_half = dot(dy_ref[...], wo_ref[...], ((1,), (1,))).astype(jnp.bfloat16)
+    width = x_ref.shape[1]
+    da_half = dot(dy_ref[...], wo_t_ref[...], ((1,), (0,))).astype(jnp.bfloat16)
+    parts = ([], [], [])
     for h in range(group):
         base = h * head_size
         lanes = slice(base, base + head_size)
         q_half = q_ref[:, lanes]
-        k_half = k_ref[:, lanes]
         q_unit = q_half.astype(jnp.float32)
-        k_unit = k_half.astype(jnp.float32)
+        k_unit = k_ref[:, lanes].astype(jnp.float32)
         da = da_half[:, lanes]
-        k_t = k_unit.T.astype(jnp.bfloat16)
         q_inv = inv_ref[0, :, h : h + 1]
         k_inv = inv_ref[0, :, group + h : group + h + 1]
         scale = sharp_ref[step * group + h] / head_size
@@ -125,41 +126,31 @@
         grad_v = dot(probs_half, da, ((1,), (0,)))
         row_dot = jnp.sum(grad_probs * probs, axis=0, keepdims=True)
         grad_scores = (probs * (grad_probs - row_dot)).astype(jnp.bfloat16)
-        dq = dot(k_t, grad_scores, ((1,), (0,))).T * scale
+        dq = dot(k_t_ref[lanes, :], grad_scores, ((1,), (0,))).T * scale
         dk = dot(grad_scores, q_half, ((1,), (0,))) * scale
         dq = q_inv * (dq - q_unit * jnp.mean(dq * q_unit, axis=-1, keepdims=True))
         dk = k_inv * (dk - k_unit * jnp.mean(dk * k_unit, axis=-1, keepdims=True))
-        dproj_ref[:, base : base + head_size] = dq.astype(jnp.bfloat16)
-        dproj_ref[:, gw + base : gw + base + head_size] = dk.astype(jnp.bfloat16)
-        dproj_ref[:, 2 * gw + base : 2 * gw + base + head_size] = grad_v.astype(jnp.bfloat16)
-    term = (
-        dot(dproj_ref[:, :gw], wq_ref[...], ((1,), (1,)))
-        + dot(dproj_ref[:, gw : 2 * gw], wk_ref[...], ((1,), (1,)))
-        + dot(dproj_ref[:, 2 * gw :], wv_ref[...], ((1,), (1,)))
-    )
-
-    @pl.when(step == 0)
-    def _():
-        acc_ref[...] = term
-
-    @pl.when(step > 0)
-    def _():
-        acc_ref[...] += term
+        for part, value in zip(parts, (dq, dk, grad_v)):
+            part.append(value.astype(jnp.bfloat16))
+    for at, part in enumerate(parts):
+        start = pl.multiple_of(at * width + step * gw, gw)
+        dproj_ref[:, pl.ds(start, gw)] = jnp.concatenate(part, axis=1)
 
     @pl.when(step == pl.num_programs(0) - 1)
     def _():
         values = x_ref[...].astype(jnp.float32)
         inv = lax.rsqrt(jnp.mean(values * values, axis=-1, keepdims=True) + epsilon)
         unit = values * inv
-        shaped = acc_ref[...] * gain_ref[...]
+        shaped = dot(dproj_ref[...], wqkv_t_ref[...], ((1,), (0,))) * gain_ref[...]
         result = dy_ref[...].astype(jnp.float32) + inv * (
             shaped - unit * jnp.mean(shaped * unit, axis=-1, keepdims=True)
         )
         gin_ref[...] = result.astype(jnp.bfloat16)
 
 
-def weights_kernel(normed_t_ref, att_ref, dproj_ref, dy_ref, gqkv_ref, gwo_ref):
-    gqkv_ref[0] = dot(normed_t_ref[...], dproj_ref[...], ((1,), (0,))).astype(jnp.bfloat16)
+def weights_kernel(normed_t_ref, att_ref, dq_ref, dk_ref, dv_ref, dy_ref, gqkv_ref, gwo_ref):
+    dproj = jnp.concatenate([dq_ref[...], dk_ref[...], dv_ref[...]], axis=1)
+    gqkv_ref[0] = dot(normed_t_ref[...], dproj, ((1,), (0,))).astype(jnp.bfloat16)
     gwo_ref[...] = dot(att_ref[...], dy_ref[...], ((1,), (0,))).astype(jnp.bfloat16)
 
 
@@ -182,6 +173,7 @@
     ]
     invs = pl.BlockSpec((1, rows, 2 * group), lambda g: (g, 0, 0))
     probs_spec = pl.BlockSpec((group, rows, rows), lambda g: (g, 0, 0))
+    w_qkv_t, w_out_t = w_qkv.T, w_out.T
     params = pltpu.CompilerParams(vmem_limit_bytes=60 * 1024 * 1024)
 
     def cost(flops):
@@ -193,11 +185,12 @@
         in_specs=[smem, whole((rows, width)), whole((1, width))]
         + weights
         + [whole((rows, 1)), whole((1, rows)), whole((rows, 1))],
-        out_specs=[whole((width, rows)), cols(gw), cols(gw), cols(gw), invs, probs_spec, lines(rows)],
+        out_specs=[whole((width, rows)), cols(gw), cols(gw), lines(rows), cols(gw), invs, probs_spec, lines(rows)],
         out_shape=[
             jax.ShapeDtypeStruct((width, rows), half),
             jax.ShapeDtypeStruct((rows, width), half),
             jax.ShapeDtypeStruct((rows, width), half),
+            jax.ShapeDtypeStruct((width, rows), half),
             jax.ShapeDtypeStruct((rows, width), half),
             jax.ShapeDtypeStruct((steps, rows, 2 * group), jnp.float32),
             jax.ShapeDtypeStruct((heads, rows, rows), half),
@@ -210,7 +203,7 @@
         compiler_params=params,
         cost_estimate=cost(40_000_000_000),
     )
-    normed_t, q, k, v, inv, probs, att = forward(
+    normed_t, q, k, k_t, v, inv, probs, att = forward(
         sharpness,
         x,
         norm_gain[None, :],
@@ -224,22 +217,39 @@
     gin, dproj = pl.pallas_call(
         functools.partial(backward_kernel, head_size, group),
         grid=(steps,),
-        in_specs=[smem, whole((rows, width)), whole((rows, width)), whole((1, width))]
-        + weights
-        + [lines(width), cols(gw), cols(gw), cols(gw), invs, probs_spec],
-        out_specs=[whole((rows, width)), cols(3 * gw)],
+        in_specs=[
+            smem,
+            whole((rows, width)),
+            whole((rows, width)),
+            whole((1, width)),
+            whole((3 * width, width)),
+            pl.BlockSpec((width, gw), lambda g: (0, g)),
+            cols(gw),
+            cols(gw),
+            lines(rows),
+            cols(gw),
+            invs,
+            probs_spec,
+        ],
+        out_specs=[whole((rows, width)), whole((rows, 3 * width))],
         out_shape=[
             jax.ShapeDtypeStruct((rows, width), half),
             jax.ShapeDtypeStruct((rows, 3 * width), half),
         ],
-        scratch_shapes=[pltpu.VMEM((rows, width), jnp.float32)],
         compiler_params=params,
         cost_estimate=cost(25_000_000_000),
-    )(sharpness, x, dy, norm_gain[None, :], w_qkv, w_qkv, w_qkv, w_out, q, k, v, inv, probs)
+    )(sharpness, x, dy, norm_gain[None, :], w_qkv_t, w_out_t, q, k, k_t, v, inv, probs)
     gqkv, gwo = pl.pallas_call(
         weights_kernel,
         grid=(steps,),
-        in_specs=[whole((width, rows)), lines(rows), cols(3 * gw), whole((rows, width))],
+        in_specs=[
+            whole((width, rows)),
+            lines(rows),
+            cols(gw),
+            pl.BlockSpec((rows, gw), lambda g: (0, steps + g)),
+            pl.BlockSpec((rows, gw), lambda g: (0, 2 * steps + g)),
+            whole((rows, width)),
+        ],
         out_specs=[pl.BlockSpec((1, width, 3 * gw), lambda g: (g, 0, 0)), lines(width)],
         out_shape=[
             jax.ShapeDtypeStruct((steps, width, 3 * gw), half),
@@ -247,7 +257,7 @@
         ],
         compiler_params=params,
         cost_estimate=cost(8_000_000_000),
-    )(normed_t, att, dproj, dy)
+    )(normed_t, att, dproj, dproj, dproj, dy)
     return gin, gqkv, gwo
 
 

time: 206 us -> 195 us (0.947)
  Pallas kernels: 120 us -> 110 us
  local copies, waits for them, and re-layouts: 17.3 us -> 24.5 us
  waiting for transfers between devices: 52.4 us -> 45.2 us
    pallas_call x1, Pallas kernels: 43.3 us -> 31.5 us  [patch_grads(): pl.pallas_call(functools.partial(backward_kernel, head_size, group), grid...]
    all_to_all x1, waiting for transfers between devices: 25 us -> 17.8 us  [layer(): lax.all_to_all(grad_out, 'dev', split_axis=1, concat_axis=0, tiled=True)]
    unnamed x18 -> x22, local copies, waits for them, and re-layouts: 11 us -> 18.2 us
  transfers between devices with their start and end apart: 3 -> 3, of which waited for: 2 -> 2; matrix products, arithmetic and copies ran while one was open for 3% -> 7% of each run, Pallas kernels for 25% -> 26%
where the time goes in v4:
time: 195 us
  Pallas kernels  110 us (56%)
  waiting for transfers between devices  45.2 us (23%)
  local copies, waits for them, and re-layouts  24.5 us (13%)
  starting transfers between devices  14.6 us (7%)
    pallas_call x1, Pallas kernels, scatter_sums(): pl.pallas_call(functools.partial(scatter_kernel, n, chunks, cols // 3), i...  42.2 us
    pallas_call x1, Pallas kernels, patch_grads(): pl.pallas_call(functools.partial(backward_kernel, head_size, group), grid...  31.5 us
    all_to_all x1, waiting for transfers between devices, layer(): lax.all_to_all(hidden_in, 'dev', split_axis=1, concat_axis=0, tiled=True)  27.4 us
    pallas_call x1, Pallas kernels, patch_grads(): forward(sharpness, x, norm_gain[None, :], w_qkv, w_qkv, w_qkv, cohort_ids...  26.8 us
    unnamed x22, local copies, waits for them, and re-layouts  18.2 us
    all_to_all x1, waiting for transfers between devices, layer(): lax.all_to_all(grad_out, 'dev', split_axis=1, concat_axis=0, tiled=True)  17.8 us
    pallas_call x1, Pallas kernels, patch_grads(): pl.pallas_call(weights_kernel, grid=(steps,), in_specs=[whole((width, row...  9 us
    all_to_all x1, starting transfers between devices, layer(): lax.all_to_all(hidden_in, 'dev', split_axis=1, concat_axis=0, tiled=True)  7.33 us
  transfers between devices with their start and end apart: 3, of which 2 were waited for; matrix products, arithmetic and copies ran while one was open for 7% of the time, Pallas kernels for 26%

profile of v4, /device:TPU:0, one launch (start us, length us, event | category | flops | bytes accessed | tf_op | source)
XLA Modules:
  0.0 194.5 jit_solution(8395209988640533395)
XLA Ops:
  0.6 2.8 %copy.24 = bf16[20,32,768]{2,0,1:T(8,128)(2,1)} copy(bf16[20,32,768]{2,1,0:T(8,128)(2,1)} %param.8) | data formatting | bytes 1966080 | tf_op args[0]
  3.4 0.0 copy-start.3
  3.4 7.3 %all-to-all-start = ((bf16[20,32,768]{2,0,1:T(8,128)(2,1)}), bf16[20,32,768]{2,0,1:T(8,128)(2,1)S(1)}, u32[]{:S(2)}, u32[]{:S(2)}) async-start(bf16[20,32,768]{2,0,1:T(8,128)(2,1)} %copy.24), calls=%async_computation | async-start | bytes 2359296 | tf_op jit(solution)/shard_map/all_to_all | solution.py:382
  10.7 0.0 copy-done.3
  10.8 1.6 copy.25
  12.3 27.4 %all-to-all-done = bf16[20,32,768]{2,0,1:T(8,128)(2,1)S(1)} async-done(((bf16[20,32,768]{2,0,1:T(8,128)(2,1)}), bf16[20,32,768]{2,0,1:T(8,128)(2,1)S(1)}, u32[]{:S(2)}, u32[]{:S(2)}) %all-to-all-start) | async-done | bytes 983072 | tf_op jit(solution)/shard_map/all_to_all | solution.py:382
  39.8 3.6 %all-to-all-start.1 = ((bf16[20,32,768]{2,0,1:T(8,128)(2,1)}), bf16[20,32,768]{2,0,1:T(8,128)(2,1)S(1)}, u32[]{:S(2)}, u32[]{:S(2)}) async-start(bf16[20,32,768]{2,0,1:T(8,128)(2,1)} %copy.25), calls=%async_computation.1 | async-start | bytes 2359296 | tf_op jit(solution)/shard_map/all_to_all | solution.py:383
  43.4 0.0 copy-done.4
  43.4 0.6 broadcast_in_dim.12.cohort_row_ref
  44.0 0.9 broadcast_in_dim.13.cohort_col_ref
  44.9 0.0 copy-done.5
  44.9 0.6 broadcast_in_dim.10.gain_ref
  45.4 0.0 copy-done.6
  45.4 0.9 copy.29.seen_ref
  46.4 0.0 copy-done.2
  46.4 1.4 copy.27
  47.8 5.8 %copy.26 = bf16[768,2304]{0,1:T(8,128)(2,1)} copy(bf16[768,2304]{1,0:T(8,128)(2,1)} %wv_ref.1) | data formatting | bytes 7077888 | tf_op args[3]
  53.6 1.0 squeeze.6.x_ref
  54.6 17.8 %all-to-all-done.1 = bf16[20,32,768]{2,0,1:T(8,128)(2,1)S(1)} async-done(((bf16[20,32,768]{2,0,1:T(8,128)(2,1)}), bf16[20,32,768]{2,0,1:T(8,128)(2,1)S(1)}, u32[]{:S(2)}, u32[]{:S(2)}) %all-to-all-start.1) | async-done | bytes 983072 | tf_op jit(solution)/shard_map/all_to_all | solution.py:383
  72.4 1.1 squeeze.7.dy_ref
  73.5 26.8 %shard_map.103 = (bf16[768,640]{1,0:T(8,128)(2,1)}, bf16[640,768]{1,0:T(8,128)(2,1)}, bf16[640,768]{1,0:T(8,128)(2,1)}, bf16[768,640]{1,0:T(8,128)(2,1)}, bf16[6...) custom-call(f32[12]{0:T(128)} %sharp_ref.3, ...), custom_call_target="tpu_custom_call" | custom-call | flops 40000000000 | bytes 9830400 | tf_op jit(solution)/shard_map/pallas_call | solution.py:206
  100.3 31.5 %shard_map.104 = (bf16[640,768]{1,0:T(8,128)(2,1)}, bf16[640,2304]{1,0:T(8,128)(2,1)}) custom-call(f32[12]{0:T(128)} %sharp_ref.3, bf16[640,768]{1,0:T(8,128)(2,1)} %squeeze.6.x_ref, bf16[640,768]{1,0:T(8,128)(2,1)} %squeeze.7.dy_ref, f32[1,768]{1,0:T(1,128)} %broadcast_in_dim.10.gain_ref, bf16[2304,768]{1,0:T(8,128)(2,1)} %bitcast.20, ...), custom_call_target="tpu_custom_call" | custom-call | flops 24999999488 | bytes 9830400 | tf_op jit(solution)/shard_map/pallas_call | solution.py:217
  131.8 2.2 %reshape.17 = bf16[32,20,768]{2,1,0:T(8,128)(2,1)} reshape(bf16[640,768]{1,0:T(8,128)(2,1)} %get-tuple-element.23) | data formatting | bytes 1966080 | tf_op jit(solution)/shard_map/reshape | solution.py:390
  134.0 3.6 %all-to-all-start.2 = ((bf16[32,20,768]{2,1,0:T(8,128)(2,1)}), bf16[32,20,768]{2,1,0:T(8,128)(2,1)S(1)}, u32[]{:S(2)}, u32[]{:S(2)}) async-start(bf16[32,20,768]{2,1,0:T(8,128)(2,1)} %reshape.17), calls=%async_computation.2 | async-start | bytes 2359296 | tf_op jit(solution)/shard_map/all_to_all | solution.py:393
  137.6 9.0 %shard_map.105 = (bf16[6,768,384]{2,1,0:T(8,128)(2,1)}, bf16[768,768]{1,0:T(8,128)(2,1)}) custom-call(bf16[768,640]{1,0:T(8,128)(2,1)} %get-tuple-element.24.normed_t_ref, bf16[768,640]{1,0:T(8,128)(2,1)} %get-tuple-element.25.att_ref, bf16[640,2304]{1,0:T(8,128)(2,1)} %get-tuple-element.26.dq_ref.dk_ref.dv_ref, ...), custom_call_target="tpu_custom_call" | custom-call | flops 8000000000 | bytes 9830400 | tf_op jit(solution)/shard_map/pallas_call | solution.py:242
  146.6 2.0 %copy-done = bf16[6,768,384]{2,1,0:T(8,128)(2,1)S(1)} copy-done((bf16[6,768,384]{2,1,0:T(8,128)(2,1)S(1)}, bf16[6,768,384]{2,1,0:T(8,128)(2,1)}, u32[]{:S(2)}) %copy-start) | copy-done | bytes 3538968
  148.6 1.3 copy-done.1
  149.9 42.2 %shard_map.106 = (f32[24,2304]{1,0:T(8,128)S(1)}, f32[24,768]{1,0:T(8,128)S(1)}) custom-call(bf16[6,2,2,2,2,2,24,384]{7,6,5,4,3,2,1,0:T(8,128)(2,1)S(1)} %bitcast.15, bf16[2,2,2,2,2,24,768]{6,5,4,3,2,1,0:T(8,128)(2,1)S(1)} %bitcast.16), custom_call_target="tpu_custom_call" | custom-call | flops 40000000000 | bytes 14155776 | tf_op jit(solution)/shard_map/pallas_call | solution.py:356
  192.1 0.0 all-to-all-done.2
  192.1 1.1 copy.30
  193.2 0.7 copy.33
  193.9 0.6 copy.34
  (6 shorter events, 0.0 us)
Async XLA Ops:
  3.4 7.3 %copy-start.3 = (bf16[20,32,768]{2,1,0:T(8,128)(2,1)S(1)}, bf16[20,32,768]{2,1,0:T(8,128)(2,1)}, u32[]{:S(2)}) copy-start(bf16[20,32,768]{2,1,0:T(8,128)(2,1)} %param.9) | copy-start | bytes 2949124
  3.4 36.3 %all-to-all-start = ((bf16[20,32,768]{2,0,1:T(8,128)(2,1)}), bf16[20,32,768]{2,0,1:T(8,128)(2,1)S(1)}, u32[]{:S(2)}, u32[]{:S(2)}) async-start(bf16[20,32,768]{2,0,1:T(8,128)(2,1)} %copy.24), calls=%async_computation | async-start | bytes 2359296 | tf_op jit(solution)/shard_map/all_to_all | solution.py:382
  12.3 31.1 %copy-start.4 = (s32[640]{0:T(1024)S(1)}, s32[640]{0:T(1024)}, u32[]{:S(2)}) copy-start(s32[640]{0:T(1024)} %param.14) | copy-start | bytes 7684
  12.3 32.5 %copy-start.5 = (f32[768]{0:T(1024)S(1)}, f32[768]{0:T(1024)}, u32[]{:S(2)}) copy-start(f32[768]{0:T(1024)} %param.10) | copy-start | bytes 9220
  12.3 33.1 %copy-start.6 = (s32[640,1]{0,1:T(1,128)S(1)}, s32[640,1]{0,1:T(1,128)}, u32[]{:S(2)}) copy-start(s32[640,1]{0,1:T(1,128)} %param.15) | copy-start | bytes 7684
  12.3 34.0 %copy-start.2 = (bf16[768,768]{1,0:T(8,128)(2,1)S(1)}, bf16[768,768]{1,0:T(8,128)(2,1)}, u32[]{:S(2)}) copy-start(bf16[768,768]{1,0:T(8,128)(2,1)} %param.12) | copy-start | bytes 3538948
  39.8 32.6 %all-to-all-start.1 = ((bf16[20,32,768]{2,0,1:T(8,128)(2,1)}), bf16[20,32,768]{2,0,1:T(8,128)(2,1)S(1)}, u32[]{:S(2)}, u32[]{:S(2)}) async-start(bf16[20,32,768]{2,0,1:T(8,128)(2,1)} %copy.25), calls=%async_computation.1 | async-start | bytes 2359296 | tf_op jit(solution)/shard_map/all_to_all | solution.py:383
  134.0 58.1 %all-to-all-start.2 = ((bf16[32,20,768]{2,1,0:T(8,128)(2,1)}), bf16[32,20,768]{2,1,0:T(8,128)(2,1)S(1)}, u32[]{:S(2)}, u32[]{:S(2)}) async-start(bf16[32,20,768]{2,1,0:T(8,128)(2,1)} %reshape.17), calls=%async_computation.2 | async-start | bytes 2359296 | tf_op jit(solution)/shard_map/all_to_all | solution.py:393
  146.6 2.0 %copy-start = (bf16[6,768,384]{2,1,0:T(8,128)(2,1)S(1)}, bf16[6,768,384]{2,1,0:T(8,128)(2,1)}, u32[]{:S(2)}) copy-start(bf16[6,768,384]{2,1,0:T(8,128)(2,1)} %get-tuple-element.27) | copy-start | bytes 10616836
  148.6 1.3 copy-start.1
